TPU v7x, 32 devices: a whole 2x2x4 slice. The times are simulated.
32 devices in a mesh: grp: 2 (over y), band: 4 (over z), sect: 4 (over x, core).
Axes of the slice: x: 2, y: 2, z: 4, core: 2. Of those that a mesh axis runs over, the one named last changes fastest.
Arguments:
- features: bfloat16 [4, 24, 96, 2048], P('grp', 'band', None, 'sect'), parts along dimension 0, may hold values from -16 to 16
- low_level: bfloat16 [4, 24, 96, 256], P('grp', 'band'), parts along dimension 0, may hold values from -6 to 6
- land_mask: int32 [4, 24], P('grp', 'band'), parts along dimension 0, may hold values from 0 to 1, as said below
- weight_one: bfloat16 [2048, 256], P('sect'), may hold values from -0.125 to 0.125
- weight_dilated: bfloat16 [3, 3, 3, 2048, 256], P(None, None, None, 'sect'), may hold values from -0.046875 to 0.046875
- bias_branch: float32 [4, 256], replicated, may hold values from -3 to 3
- weight_pool: bfloat16 [2048, 256], P('sect'), may hold values from -0.125 to 0.125
- bias_pool: float32 [256], replicated, may hold values from -3 to 3
- weight_project: bfloat16 [1280, 256], replicated, may hold values from -0.15625 to 0.15625
- bias_project: float32 [256], replicated, may hold values from -3 to 3
- weight_reduce: bfloat16 [256, 48], replicated, may hold values from -0.375 to 0.375
- bias_reduce: float32 [48], replicated, may hold values from -3 to 3
- weight_merging: bfloat16 [3, 3, 304, 256], replicated, may hold values from -0.109375 to 0.109375
- bias_merging: float32 [256], replicated, may hold values from -3 to 3
Outputs:
- merged_map: bfloat16 [4, 24, 96, 256], P('grp', 'band'), parts along dimension 0
There are 2 independent parts, one for each index of `grp`. A program takes and returns all parts, laid end to end along the dimension named above; an argument that names none is the same for every part. Nothing has to cross between parts.
Inputs may be any that keep to these rules, and one draw needn't show every extreme that they name: `land_mask`: in every image each aligned block of 6 rows holds at most 4 ones and at least 2 ones, its first and last rows always being ones; in every image some block holds exactly 4.
All inputs are finite; a program needn't handle non-finite values.
Results may differ from a plain program's by a relative error of at most 0.012.
Values may be sent and summed in bfloat16 or wider, within the bound.
A program may use at most 64 MiB of HBM per device.

v0:
```python
import functools

import jax
import jax.numpy as jnp
from jax import lax
from jax.experimental import pallas as pl
from jax.experimental.pallas import tpu as pltpu
from jax.sharding import PartitionSpec as P

DILATIONS = (12, 24, 36)
LAND_BLOCK = 6
LAND_MOST = 4
PRECISE = lax.Precision.HIGHEST
MESH = pl.DeviceIdType.MESH
F32 = jnp.float32
BF16 = jnp.bfloat16


def plan(rows, bands):
    off = []
    for k in (1, 2, 3):
        d = DILATIONS[k - 1]
        assert d % rows == 0
        hop = d // rows
        if hop < bands:
            off.append((k, 0, hop))
            off.append((k, 2, hop))
    order = [3, 2, 0, 1]
    return off, order


def kernel(
    dims, mask, feat_h, low_h, w1_h, wd_h, bbr, wpool_h, bpool, wproj_h, bproj, wr, br, wm_h, bm,
    out,
    feat, low, low_halo, w1, wd, wpool, wproj, wmp, wml, comp, m_l, m_r,
    part_off, crecv_off, xsend_off, xrecv_off, zsend, zrecv,
    part_own, crecv_own, xsend_own, xrecv_own, keep_off, keep_own,
    sums, pool_s, pool_b, gath, gath_b, halo, joined, lowred, lowacc, outc,
    loc_sem, lo_s, lo_r, c_s, c_r, x_s, x_r, z_s, z_r, ps_s, ps_r, pb_s, pb_r,
    gx_s, gx_r, gc_s, gc_r, hx_s, hx_r, hc_s, hc_r,
):
    mb, rows, cols, ch, br_w, live, nb, ns, low_w, lowp = dims
    nx = ns // 2
    cs = cols // nx
    off, order = plan(rows, nb)
    n_off = len(off)
    need = [(k, 1) for k in order if k] + [(k, i) for k, i, _ in off]
    pad = (m_l.shape[1] - cols) // 2

    band = lax.axis_index("band")
    sect = lax.axis_index("sect")
    core = lax.rem(sect, 2)
    xi = lax.div(sect, 2)

    locals_ = {}

    def fetch(name, src, dst):
        c = pltpu.make_async_copy(src, dst, loc_sem.at[len(locals_)])
        locals_[name] = c
        c.start()

    fetch("feat", feat_h, feat)
    for k, i, _ in off:
        fetch((k, i), wd_h.at[k - 1, i], wd.at[need.index((k, i))])
    fetch("wpool", wpool_h, wpool)
    for k in order:
        if k:
            fetch((k, 1), wd_h.at[k - 1, 1], wd.at[need.index((k, 1))])
        else:
            fetch("w1", w1_h, w1)
    fetch("low", low_h, low)
    fetch("wproj", wproj_h, wproj)
    fetch("wml", wm_h.at[:, :, pl.ds(br_w, lowp)], wml)
    for i in range(3):
        for j in range(3):
            fetch(("wmp", i, j), wm_h.at[i, j, pl.ds(0, br_w)], wmp.at[j, pl.ds(i * br_w, br_w)])

    bar = pltpu.get_barrier_semaphore()
    up_ok = band >= 1
    dn_ok = band + 1 < nb

    def hello(b, s):
        pl.semaphore_signal(bar, inc=1, device_id={"band": b, "sect": s}, device_id_type=MESH)

    for e in range(1, ns):
        hello(band, lax.rem(sect + e, ns))
    for e in range(1, nb):
        hello(lax.rem(band + e, nb), sect)
    for ok, step in ((up_ok, -1), (dn_ok, 1)):
        @pl.when(ok)
        def _(step=step):
            for e in range(1, nx):
                hello(band + step, lax.rem(sect + 2 * e, ns))
    def rcopy(src, dst, s, r, **where):
        return pltpu.make_async_remote_copy(
            src_ref=src, dst_ref=dst, send_sem=s, recv_sem=r, device_id=where, device_id_type=MESH
        )

    low_up = rcopy(low_h.at[:, 0], low_halo.at[1], lo_s.at[0], lo_r.at[1], band=band - 1, sect=sect)
    low_dn = rcopy(
        low_h.at[:, rows - 1], low_halo.at[0], lo_s.at[1], lo_r.at[0], band=band + 1, sect=sect
    )

    def slots(m):
        on = [mask[m, y] for y in range(rows)]
        slot_of = [jnp.int32(0)] + [None] * (rows - 2) + [jnp.int32(live - 1)]
        row_of = [jnp.int32(0)] * live
        row_of[live - 1] = jnp.int32(rows - 1)
        held = [jnp.int32(0)] * live
        held[0] = on[0]
        held[live - 1] = on[rows - 1]
        count = jnp.int32(0)
        for y in range(1, rows - 1):
            slot_of[y] = jnp.where(on[y] > 0, jnp.minimum(count + 1, live - 1), 0)
            for r in range(1, live - 1):
                hit = jnp.logical_and(on[y] > 0, count == r - 1)
                row_of[r] = jnp.where(hit, y, row_of[r])
                held[r] = jnp.where(hit, 1, held[r])
            count = count + on[y]
        return on, slot_of, row_of, held

    for ref in (m_l, m_r):
        zero = jnp.zeros((ref.shape[0], pad, br_w), F32)
        ref[:, :pad] = zero
        ref[:, pad + cols :] = zero
    for at in (0, rows + 1):
        joined[:, at] = jnp.zeros((mb, cols, br_w), BF16)

    locals_["feat"].wait()

    def taps(lhs, n, wref, d):
        mid = jnp.dot(lhs, wref[1], preferred_element_type=F32).reshape(n, cols, br_w)
        m_l[:n, pl.ds(pad, cols)] = jnp.dot(
            lhs, wref[0], preferred_element_type=F32
        ).reshape(n, cols, br_w)
        m_r[:n, pl.ds(pad, cols)] = jnp.dot(
            lhs, wref[2], preferred_element_type=F32
        ).reshape(n, cols, br_w)
        return mid + m_l[:n, pl.ds(pad - d, cols)] + m_r[:n, pl.ds(pad + d, cols)]

    def core_copy(t):
        if t < n_off:
            src, dst = part_off.at[t, 0], crecv_off.at[t]
        else:
            src, dst = part_own.at[t - n_off, 0], crecv_own.at[t - n_off]
        return rcopy(src, dst, c_s.at[t], c_r.at[t], sect=xi * 2 + 1 - core)

    def x_copy(t, e, incoming=False):
        send, recv, u = (
            (xsend_off, xrecv_off, t) if t < n_off else (xsend_own, xrecv_own, t - n_off)
        )
        other = lax.rem(xi + e, nx)
        slot = other if incoming else xi
        return rcopy(
            send.at[u, other], recv.at[u, slot], x_s.at[t, other], x_r.at[t, slot],
            sect=other * 2 + core,
        )

    def first(t):
        def body(step, carry):
            image = jnp.where(step == 0, 1 - core, core)
            if t < n_off:
                k, i, _ = off[t]
                lhs = feat[image].reshape(rows * cols, ch)
                val = taps(lhs, rows, wd.at[need.index((k, i))], DILATIONS[k - 1])
                part_off[t, step] = val.astype(BF16)
            else:
                k = order[t - n_off]
                lhs = comp[image].reshape(live * cols, ch)
                if k:
                    val = taps(lhs, live, wd.at[need.index((k, 1))], DILATIONS[k - 1])
                else:
                    val = jnp.dot(lhs, w1[...], preferred_element_type=F32).reshape(
                        live, cols, br_w
                    )
                part_own[t - n_off, step] = val.astype(BF16)

            if t >= n_off:
                @pl.when(step == 0)
                def _():
                    core_copy(t).start()
            return carry

        lax.fori_loop(0, 2, body, 0)

    def second(t):
        core_copy(t).wait_recv()
        part, got, send, keep, u = (
            (part_off, crecv_off, xsend_off, keep_off, t)
            if t < n_off
            else (part_own, crecv_own, xsend_own, keep_own, t - n_off)
        )
        for c in range(nx):
            cell = pl.ds(c * cs, cs)
            total = part[u, 1, :, cell].astype(F32) + got[u, :, cell].astype(F32)
            send[u, c] = total.astype(BF16)

            @pl.when(xi == c)
            def _():
                keep[u] = total
        for e in range(1, nx):
            x_copy(t, e).start()

    def shared(t):
        recv, keep, u = (
            (xrecv_off, keep_off, t) if t < n_off else (xrecv_own, keep_own, t - n_off)
        )
        total = keep[u]
        for e in range(1, nx):
            x_copy(t, e, True).wait_recv()
            total = total + recv[u, lax.rem(xi + e, nx)].astype(F32)
        return total

    def sends_to(t):
        k, i, hop = off[t]
        return band + hop < nb if i == 0 else band - hop >= 0

    def gets_from(t):
        k, i, hop = off[t]
        return band - hop >= 0 if i == 0 else band + hop < nb

    def z_copy(t):
        k, i, hop = off[t]
        return rcopy(
            zsend.at[t], zrecv.at[t], z_s.at[t], z_r.at[t],
            band=band + hop if i == 0 else band - hop, sect=sect,
        )

    def third_off(t):
        zsend[t] = shared(t).astype(BF16)
        z_copy(t).start()

    def guarded(fn, t):
        @pl.when(sends_to(t))
        def _():
            fn(t)

    for t in range(n_off):
        locals_[off[t][:2]].wait()
        guarded(first, t)

    sides_held = jnp.minimum(band, 1) + jnp.minimum(nb - 1 - band, 1)
    pl.semaphore_wait(bar, (ns - 1) + (nb - 1) + (nx - 1) * sides_held)

    for t in range(n_off):
        guarded(lambda t: core_copy(t).start(), t)
    @pl.when(up_ok)
    def _():
        low_up.start()

    @pl.when(dn_ok)
    def _():
        low_dn.start()

    sums[...] = jnp.zeros_like(sums)
    locals_["wpool"].wait()
    for m in range(mb):
        acc = jnp.zeros((cols, ch), F32)
        for y in range(rows):
            acc = acc + feat[m, y].astype(F32)
        sums[m : m + 1, :] = jnp.sum(acc, axis=0, keepdims=True)
    pool_s[sect] = jnp.dot(
        sums[...], wpool[...].astype(F32), precision=PRECISE, preferred_element_type=F32
    )

    def pool_sect(e, incoming=False):
        other = lax.rem(sect + e, ns)
        slot = other if incoming else sect
        return rcopy(
            pool_s.at[sect], pool_s.at[slot], ps_s.at[other], ps_r.at[slot], sect=other
        )

    def pool_band(e, incoming=False):
        other = lax.rem(band + e, nb)
        slot = other if incoming else band
        return rcopy(
            pool_b.at[band], pool_b.at[slot], pb_s.at[other], pb_r.at[slot], band=other
        )

    for e in range(1, ns):
        pool_sect(e).start()

    facts = [slots(m) for m in range(mb)]
    for m in range(mb):
        for r in range(live):
            comp[m, r] = feat[m, facts[m][2][r]]

    for t in range(n_off):
        guarded(second, t)

    t0 = n_off

    def own(u):
        locals_[(order[u], 1) if order[u] else "w1"].wait()
        first(t0 + u)

    own(0)
    own(1)
    second(t0)
    for e in range(1, ns):
        pool_sect(e, True).wait_recv()
    total = pool_s[0]
    for s in range(1, ns):
        total = total + pool_s[s]
    pool_b[band] = total
    for e in range(1, nb):
        pool_band(e).start()

    own(2)
    second(t0 + 1)
    own(3)
    second(t0 + 2)
    for t in range(n_off):
        guarded(third_off, t)
    second(t0 + 3)

    locals_["low"].wait()
    locals_["wml"].wait()

    def reduced(v):
        return jax.nn.relu(
            lax.dot_general(
                v, wr[...], (((1,), (1,)), ((), ())), preferred_element_type=F32
            )
            + br[...]
        ).astype(BF16)

    for m in range(mb):
        lowred[m, 1 : rows + 1] = reduced(low[m].reshape(rows * cols, low_w)).reshape(
            rows, cols, lowp
        )
    for side, at, ok, copy in ((0, 0, up_ok, low_dn), (1, rows + 1, dn_ok, low_up)):
        @pl.when(ok)
        def _(side=side, at=at, copy=copy):
            copy.wait_recv()
            for m in range(mb):
                lowred[m, at] = reduced(low_halo[side, m])

        @pl.when(jnp.logical_not(ok))
        def _(at=at):
            for m in range(mb):
                lowred[m, at] = jnp.zeros((cols, lowp), BF16)

    def stash(terms):
        for ref, term in zip((m_l, m_r), (terms[0], terms[2])):
            ref[:live, pl.ds(pad, cols)] = term.reshape(live, cols, br_w)
        outc[...] = terms[1].reshape(live, cols, br_w)

    def combined():
        return outc[...] + m_l[:live, pl.ds(pad - 1, cols)] + m_r[:live, pl.ds(pad + 1, cols)]

    for m in range(mb):
        row_of = facts[m][2]
        terms = [None] * 3
        for i in range(3):
            lhs = jnp.concatenate([lowred[m, row_of[r] + i] for r in range(live)], axis=0)
            for j in range(3):
                term = jnp.dot(lhs, wml[i, j], preferred_element_type=F32)
                terms[j] = term if i == 0 else terms[j] + term
        stash(terms)
        lowacc[m] = combined() + bm[...].reshape(1, 1, br_w)

    locals_["wproj"].wait()
    for e in range(1, nb):
        pool_band(e, True).wait_recv()
    total = pool_b[0]
    for b in range(1, nb):
        total = total + pool_b[b]
    pooled = jax.nn.relu(total / (nb * rows * cols) + bpool[...])
    context = jnp.dot(
        pooled, wproj[4 * br_w :].astype(F32), precision=PRECISE, preferred_element_type=F32
    )
    mine = context[0:1]
    for m in range(1, mb):
        mine = jnp.where(core == m, context[m : m + 1], mine)
    base = mine + bproj[...]

    _, _, own_row, own_held = slots(core)
    acc = jnp.zeros((live * cs, br_w), F32)
    for u, k in enumerate(order):
        keep_own[u] = shared(t0 + u)
        for t in range(n_off):
            if off[t][0] == k:
                @pl.when(gets_from(t))
                def _(t=t, u=u):
                    z_copy(t).wait_recv()
                    for r in range(live):
                        keep_own[u, r] = keep_own[u, r] + zrecv[t, own_row[r]].astype(F32)
        branch = jax.nn.relu(keep_own[u] + bbr[k : k + 1].reshape(1, 1, br_w)).astype(BF16)
        acc = acc + jnp.dot(
            branch.reshape(live * cs, br_w), wproj[k * br_w : (k + 1) * br_w],
            preferred_element_type=F32,
        )
    done = jax.nn.relu(acc + base).reshape(live, cs, br_w)
    for r in range(live):
        gath[xi, r] = (done[r] * own_held[r].astype(F32)).astype(BF16)

    peer = xi * 2 + 1 - core

    def gather_x(e, incoming=False):
        other = lax.rem(xi + e, nx)
        slot = other if incoming else xi
        return rcopy(
            gath.at[xi], gath.at[slot], gx_s.at[other], gx_r.at[slot], sect=other * 2 + core
        )

    def gather_core(c):
        return rcopy(gath.at[c], gath_b.at[c], gc_s.at[c], gc_r.at[c], sect=peer)

    def halo_x(side, e, incoming=False):
        other = lax.rem(xi + e, nx)
        slot = other if incoming else xi
        src = gath.at[xi, live - 1 if side == 0 else 0]
        return rcopy(
            src, halo.at[side, slot * 2 + core], hx_s.at[side, other], hx_r.at[side, slot],
            band=band + 1 if side == 0 else band - 1, sect=other * 2 + core,
        )

    def halo_core(side, c, incoming=False):
        cell = c * 2 + (1 - core if incoming else core)
        return rcopy(
            halo.at[side, cell], halo.at[side, cell], hc_s.at[side, c], hc_r.at[side, c], sect=peer
        )

    for e in range(1, nx):
        gather_x(e).start()
    for side, ok in ((0, dn_ok), (1, up_ok)):
        @pl.when(ok)
        def _(side=side):
            for e in range(nx):
                halo_x(side, e).start()
    gather_core(xi).start()
    for i in range(3):
        for j in range(3):
            locals_[("wmp", i, j)].wait()
    for e in range(1, nx):
        gather_x(e, True).wait_recv()
        gather_core(lax.rem(xi + e, nx)).start()

    for step in range(2):
        image = core if step == 0 else 1 - core
        on, slot_of, row_of, _ = slots(image)
        cells = gath if step == 0 else gath_b
        if step == 1:
            for c in range(nx):
                gather_core(c).wait_recv()
        for y in range(rows):
            for c in range(nx):
                joined[image, y + 1, pl.ds(c * cs, cs)] = (
                    cells[c, slot_of[y]].astype(F32) * on[y].astype(F32)
                ).astype(BF16)
        lhs = jnp.concatenate(
            [
                jnp.concatenate([joined[image, row_of[r] + i] for r in range(live)], axis=0)
                for i in range(3)
            ],
            axis=1,
        )
        stash([jnp.dot(lhs, wmp[j], preferred_element_type=F32) for j in range(3)])
        for side, ok in ((0, up_ok), (1, dn_ok)):
            @pl.when(ok)
            def _(side=side, step=step, image=image):
                for e in range(nx):
                    if step == 0:
                        halo_x(side, e, True).wait_recv()
                        halo_core(side, lax.rem(xi + e, nx)).start()
                    else:
                        halo_core(side, e, True).wait_recv()
                edge = jnp.concatenate([halo[side, c * 2 + image] for c in range(nx)], axis=0)
                at = 0 if side == 0 else live - 1
                tap = pl.ds(2 * br_w * side, br_w)
                add = [
                    jnp.dot(edge, wmp[j, tap], preferred_element_type=F32) for j in range(3)
                ]
                m_l[at, pl.ds(pad, cols)] = m_l[at, pl.ds(pad, cols)] + add[0]
                outc[at] = outc[at] + add[1]
                m_r[at, pl.ds(pad, cols)] = m_r[at, pl.ds(pad, cols)] + add[2]
        outc[...] = jax.nn.relu(combined() + lowacc[image])
        for y in range(rows):
            out[image, y] = outc[slot_of[y]].astype(BF16)

    @pl.when(up_ok)
    def _():
        low_up.wait_send()

    @pl.when(dn_ok)
    def _():
        low_dn.wait_send()

    def left(t):
        core_copy(t).wait_send()
        for e in range(1, nx):
            x_copy(t, e).wait_send()

    for t in range(n_off):
        guarded(left, t)
        guarded(lambda t: z_copy(t).wait_send(), t)
    for u in range(4):
        left(t0 + u)
    for e in range(1, ns):
        pool_sect(e).wait_send()
    for e in range(1, nb):
        pool_band(e).wait_send()
    for e in range(1, nx):
        gather_x(e).wait_send()
    for c in range(nx):
        gather_core(c).wait_send()
    for side, ok in ((0, dn_ok), (1, up_ok)):
        @pl.when(ok)
        def _(side=side):
            for e in range(nx):
                halo_x(side, e).wait_send()
    for side, ok in ((0, up_ok), (1, dn_ok)):
        @pl.when(ok)
        def _(side=side):
            for c in range(nx):
                halo_core(side, c).wait_send()


def shards(
    features, low_level, land_mask, weight_one, weight_dilated, bias_branch, weight_pool,
    bias_pool, weight_project, bias_project, weight_reduce, bias_reduce, weight_merging,
    bias_merging,
):
    mb, rows, cols, ch = features.shape
    br_w = weight_project.shape[1]
    low_w, lowp = weight_reduce.shape
    nb, ns = lax.axis_size("band"), lax.axis_size("sect")
    nx = ns // 2
    cs = cols // nx
    assert mb == 2 and ns % 2 == 0
    live = rows // LAND_BLOCK * LAND_MOST if rows % LAND_BLOCK == 0 else rows
    off, order = plan(rows, nb)
    n_off = max(len(off), 1)
    n_all = len(off) + 4
    pad = -(-max(DILATIONS) // 8) * 8
    vm, dma = pltpu.VMEM, pltpu.SemaphoreType.DMA
    dims = (mb, rows, cols, ch, br_w, live, nb, ns, low_w, lowp)
    scratch = [
        vm(features.shape, BF16),
        vm(low_level.shape, BF16),
        vm((2, mb, cols, low_w), BF16),
        vm(weight_one.shape, BF16),
        vm((3 + len(off), 3, ch, br_w), BF16),
        vm(weight_pool.shape, BF16),
        vm(weight_project.shape, BF16),
        vm((3, 3 * br_w, weight_merging.shape[3]), BF16),
        vm((3, 3, lowp, weight_merging.shape[3]), BF16),
        vm((mb, live, cols, ch), BF16),
        vm((rows, cols + 2 * pad, br_w), F32),
        vm((rows, cols + 2 * pad, br_w), F32),
        vm((n_off, 2, rows, cols, br_w), BF16),
        vm((n_off, rows, cols, br_w), BF16),
        vm((n_off, nx, rows, cs, br_w), BF16),
        vm((n_off, nx, rows, cs, br_w), BF16),
        vm((n_off, rows, cs, br_w), BF16),
        vm((n_off, rows, cs, br_w), BF16),
        vm((4, 2, live, cols, br_w), BF16),
        vm((4, live, cols, br_w), BF16),
        vm((4, nx, live, cs, br_w), BF16),
        vm((4, nx, live, cs, br_w), BF16),
        vm((n_off, rows, cs, br_w), F32),
        vm((4, live, cs, br_w), F32),
        vm((8, ch), F32),
        vm((ns, 8, br_w), F32),
        vm((nb, 8, br_w), F32),
        vm((nx, live, cs, br_w), BF16),
        vm((nx, live, cs, br_w), BF16),
        vm((2, ns, cs, br_w), BF16),
        vm((mb, rows + 2, cols, br_w), BF16),
        vm((mb, rows + 2, cols, lowp), BF16),
        vm((mb, live, cols, br_w), F32),
        vm((live, cols, br_w), F32),
        dma((19 + len(off),)),
        dma((2,)),
        dma((2,)),
        dma((n_all,)),
        dma((n_all,)),
        dma((n_all, nx)),
        dma((n_all, nx)),
        dma((n_off,)),
        dma((n_off,)),
        dma((ns,)),
        dma((ns,)),
        dma((nb,)),
        dma((nb,)),
        dma((nx,)),
        dma((nx,)),
        dma((nx,)),
        dma((nx,)),
        dma((2, nx)),
        dma((2, nx)),
        dma((2, nx)),
        dma((2, nx)),
    ]
    anym = pl.BlockSpec(memory_space=pl.ANY)
    vmem = pl.BlockSpec(memory_space=pltpu.VMEM)
    smem = pl.BlockSpec(memory_space=pltpu.SMEM)
    merged_map = pl.pallas_call(
        functools.partial(kernel, dims),
        out_shape=jax.ShapeDtypeStruct((mb, rows, cols, weight_merging.shape[3]), BF16),
        in_specs=[
            smem, anym, anym, anym, anym, vmem, anym, vmem, anym, vmem, vmem, vmem, anym, vmem,
        ],
        out_specs=vmem,
        scratch_shapes=scratch,
        compiler_params=pltpu.CompilerParams(
            collective_id=0, has_side_effects=True, vmem_limit_bytes=60 * 1024 * 1024
        ),
    )(
        land_mask, features, low_level, weight_one, weight_dilated, bias_branch, weight_pool,
        bias_pool.reshape(1, -1), weight_project, bias_project.reshape(1, -1), weight_reduce.T,
        bias_reduce.reshape(1, -1), weight_merging, bias_merging.reshape(1, -1),
    )
    return jnp.where(land_mask[:, :, None, None] != 0, merged_map, jnp.zeros_like(merged_map))


def solution(mesh):
    in_specs = (
        P("grp", "band", None, "sect"),
        P("grp", "band", None, None),
        P("grp", "band"),
        P("sect", None),
        P(None, None, None, "sect", None),
        P(),
        P("sect", None),
        P(),
        P(),
        P(),
        P(),
        P(),
        P(),
        P(),
    )
    out_specs = P("grp", "band", None, None)
    return jax.shard_map(shards, mesh=mesh, in_specs=in_specs, out_specs=out_specs, check_vma=False)
```

profile of v0, /device:TPU:0, one launch (start us, length us, event | category | flops | bytes accessed | tf_op | source)
XLA Modules:
  0.0 32.9 jit_solution(17045867777041500432)
XLA Ops:
  0.0 0.7 %broadcast_compare_fusion = pred[2,6]{1,0:T(4,128)(4,1)S(1)} fusion(s32[2,6]{1,0:T(2,128)} %mask.1), kind=kLoop, calls=%fused_computation.1 | loop fusion | flops 12 | bytes 60 | tf_op jit(solution)/shard_map/ne | solution.py:615
  0.7 30.3 %shard_map.136 = bf16[2,6,96,256]{3,2,1,0:T(8,128)(2,1)} custom-call(s32[2,6]{1,0:T(2,128)} %mask.1, bf16[2,6,96,512]{3,2,1,0:T(8,128)(2,1)} %feat_h.1, bf16[2,6,96,256]{3,2,1,0:T(8,128)(2,1)} %low_h.1, bf16[512,256]{1,0:T(8,128)(2,1)} %w1_h.1, bf16[3,3,3,512,256]{4,3,2,1,0:T(8,128)(2,1)} %wd_h.1, f32[4,256]{1,0:T(4,128)} %bbr.1, bf16[512,256]{1,0:T(8,128)(2,1)} %wpool_h.1, ...), custom_call_target="tpu_custom_call" | custom-call | tf_op jit(solution)/shard_map/pallas_call | solution.py:599
  31.0 2.0 %broadcast_select_fusion = bf16[2,6,96,256]{3,2,1,0:T(8,128)(2,1)} fusion(bf16[2,6,96,256]{3,2,1,0:T(8,128)(2,1)} %shard_map.136, pred[2,6]{1,0:T(4,128)(4,1)S(1)} %broadcast_compare_fusion), kind=kLoop, calls=%fused_computation | loop fusion | flops 294912 | bytes 1179660 | tf_op jit(solution)/shard_map/jit(_where)/select_n | solution.py:615
where the time goes:
time: 33.2 us; the launch traced here: 32.9 us
  Pallas kernels  30.3 us (91%)
  other arithmetic  2.67 us (8%)
    pallas_call x1, Pallas kernels, shards(): pl.pallas_call(functools.partial(kernel, dims), out_shape=jax.ShapeDtypeS...  30.3 us
    select_n x1, other arithmetic, shards(): jnp.where(land_mask[:, :, None, None] != 0, merged_map, jnp.zeros_like(me...  1.99 us
    ne x1, other arithmetic, shards(): land_mask[:, :, None, None] != 0  0.68 us

commit v1 on v0

v1 whole, which is shorter than its diff:
```python
import functools
import types

import jax
import jax.numpy as jnp
from jax import lax
from jax.experimental import pallas as pl
from jax.experimental.pallas import tpu as pltpu
from jax.sharding import PartitionSpec as P

DILATIONS = (12, 24, 36)
LAND_BLOCK = 6
LAND_MOST = 4
MESH = pl.DeviceIdType.MESH
F32 = jnp.float32
BF16 = jnp.bfloat16
ORDER = (3, 2, 0, 1)


def offsets(rows, bands):
    off = []
    for k in (1, 2, 3):
        d = DILATIONS[k - 1]
        assert d % rows == 0
        hop = d // rows
        if hop < bands:
            off.append((k, 0, hop))
            off.append((k, 2, hop))
    return off


def pieces(live):
    inner = live - 2
    cuts = [(0, 2)]
    if inner > 1:
        cuts += [(2, inner - inner // 2), (live - inner // 2, inner // 2)]
    elif inner:
        cuts.append((2, inner))
    return cuts


def kernel(dims, names, *refs):
    r = types.SimpleNamespace(**dict(zip(names, refs, strict=True)))
    mb, rows, cols, ch, br_w, live, nb, ns, low_w, lowp = dims
    nx = ns // 2
    cs = cols // nx
    off = offsets(rows, nb)
    n_off = len(off)
    cuts = pieces(live)
    n_cut = len(cuts)
    off_cuts = [(0, 2), (2, rows - 2)]
    need = [(k, 1) for k in ORDER if k] + [(k, i) for k, i, _ in off]
    pad = (r.m_l.shape[1] - cols) // 2
    scope = jax.named_scope

    band = lax.axis_index("band")
    sect = lax.axis_index("sect")
    core = lax.rem(sect, 2)
    xi = lax.div(sect, 2)
    mine, theirs = core, 1 - core
    peer = xi * 2 + 1 - core

    waits = {}

    def fetch(name, *copies, whole):
        sem = r.loc_sem.at[len(waits)]
        for src, dst in copies:
            pltpu.make_async_copy(src, dst, sem).start()
        waits[name] = pltpu.make_async_copy(whole, whole, sem)

    def need_now(*which):
        for name in which:
            waits[name].wait()

    def taps_of(k, i):
        return r.wd_h.at[k - 1, i], r.wd.at[need.index((k, i))]

    fetch("mask", (r.mask_h, r.mask), whole=r.mask)
    fetch("theirs", (r.feat_h.at[theirs], r.feat.at[0]), whole=r.feat.at[0])
    fetch("first", taps_of(*need[0]), whole=r.wd.at[0])
    fetch("mine", (r.feat_h.at[mine], r.feat_own), whole=r.feat_own)
    fetch(
        "wide", (r.wpool_h, r.wide.at[0]), (r.w1_h, r.wide.at[1]), whole=r.wide
    )
    if n_off:
        fetch("off", *[taps_of(*n) for n in need[3:]], whole=r.wd.at[pl.ds(3, n_off)])
    fetch("rest", *[taps_of(*n) for n in need[1:3]], whole=r.wd.at[pl.ds(1, 2)])
    fetch("low", (r.low_h.at[mine], r.low), whole=r.low)
    fetch("wr", (r.wr_h, r.wr), whole=r.wr)
    fetch("br", (r.br_h, r.br), whole=r.br)
    fetch("wml", (r.wm_h.at[:, :, pl.ds(br_w, lowp)], r.wml), whole=r.wml)
    fetch(
        "vec", (r.bm_h, r.vec.at[0]), (r.bpool_h, r.vec.at[1]), (r.bproj_h, r.vec.at[2]),
        whole=r.vec,
    )
    fetch("wproj", (r.wproj_h, r.wproj), whole=r.wproj)
    fetch("bbr", (r.bbr_h, r.bbr), whole=r.bbr)
    fetch(
        "wmp",
        *[
            (r.wm_h.at[i, j, pl.ds(0, br_w)], r.wmp.at[j, pl.ds(i * br_w, br_w)])
            for i in range(3) for j in range(3)
        ],
        whole=r.wmp,
    )

    bar = pltpu.get_barrier_semaphore()
    up_ok = band >= 1
    dn_ok = band + 1 < nb

    def hello(b, s):
        pl.semaphore_signal(bar, inc=1, device_id={"band": b, "sect": s}, device_id_type=MESH)

    for e in range(1, ns):
        hello(band, lax.rem(sect + e, ns))
    for e in range(1, nb):
        hello(lax.rem(band + e, nb), sect)

    def rcopy(src, dst, s, rs, **where):
        return pltpu.make_async_remote_copy(
            src_ref=src, dst_ref=dst, send_sem=s, recv_sem=rs, device_id=where, device_id_type=MESH
        )

    low_up = rcopy(
        r.low_h.at[mine, 0], r.low_halo.at[1], r.lo_s.at[0], r.lo_r.at[1], band=band - 1, sect=sect
    )
    low_dn = rcopy(
        r.low_h.at[mine, rows - 1], r.low_halo.at[0], r.lo_s.at[1], r.lo_r.at[0],
        band=band + 1, sect=sect,
    )

    def slots(m):
        on = [r.mask[m, y] for y in range(rows)]
        place_of = [0] + [None] * (rows - 2) + [1]
        row_of = [0, rows - 1] + [jnp.int32(0)] * (live - 2)
        count = jnp.int32(0)
        for y in range(1, rows - 1):
            place_of[y] = jnp.where(on[y] > 0, jnp.minimum(count + 2, live - 1), 0)
            for p in range(2, live):
                hit = jnp.logical_and(on[y] > 0, count == p - 2)
                row_of[p] = jnp.where(hit, y, row_of[p])
            count = count + on[y]
        return on, place_of, row_of

    for ref in (r.m_l, r.m_r):
        zero = jnp.zeros((ref.shape[0], pad, br_w), F32)
        ref[:, :pad] = zero
        ref[:, pad + cols :] = zero
    for at in (0, rows + 1):
        r.joined[at] = jnp.zeros((cols, br_w), BF16)

    def taps(lhs, n, wref, d):
        mid = jnp.dot(lhs, wref[1], preferred_element_type=F32).reshape(n, cols, br_w)
        r.m_l[:n, pl.ds(pad, cols)] = jnp.dot(
            lhs, wref[0], preferred_element_type=F32
        ).reshape(n, cols, br_w)
        r.m_r[:n, pl.ds(pad, cols)] = jnp.dot(
            lhs, wref[2], preferred_element_type=F32
        ).reshape(n, cols, br_w)
        return mid + r.m_l[:n, pl.ds(pad - d, cols)] + r.m_r[:n, pl.ds(pad + d, cols)]

    def core_copy(t):
        if t < 4:
            src, dst = r.part_own.at[t, 0], r.crecv_own.at[t]
        else:
            src, dst = r.part_off.at[t - 4, 0], r.crecv_off.at[t - 4]
        return rcopy(src, dst, r.c_s.at[max(t - 3, 0)], r.c_r.at[t], sect=peer)

    def run_of(t, g):
        return cuts[g] if t < 4 else off_cuts[g]

    def x_copy(t, g, e, incoming=False):
        lo, n = run_of(t, g)
        at = g * 2 + t // 3 if t < 4 else 2 * n_cut + (t - 4) * 2 + g
        send, recv, u = (
            (r.xsend_own, r.xrecv_own, t) if t < 4 else (r.xsend_off, r.xrecv_off, t - 4)
        )
        other = lax.rem(xi + e, nx)
        slot = other if incoming else xi
        return rcopy(
            send.at[u, other, pl.ds(lo, n)], recv.at[u, slot, pl.ds(lo, n)],
            r.x_s.at[max(t - 3, 0)], r.x_r.at[at, (e if incoming else nx - e) - 1],
            sect=other * 2 + core,
        )

    def x_arrived(g):
        for e in range(1, nx):
            whole = r.xrecv_own.at[pl.ds(0, 3), lax.rem(xi + e, nx), pl.ds(*cuts[g])]
            arrived(whole, r.x_r.at[g * 2, e - 1])

    def send_x(t, g):
        for e in range(1, nx):
            x_copy(t, g, e).start()

    def first(t, step):
        image = r.feat.at[0] if step == 0 else r.feat_own
        if t < 4:
            k = ORDER[t]
            row_of = facts[step][2]
            lhs = jnp.concatenate([image[row_of[p]] for p in range(live)], axis=0)
            if k:
                val = taps(lhs, live, r.wd.at[need.index((k, 1))], DILATIONS[k - 1])
            else:
                val = jnp.dot(lhs, r.wide[1], preferred_element_type=F32).reshape(live, cols, br_w)
            r.part_own[t, step] = val.astype(BF16)
        else:
            k, i, _ = off[t - 4]
            lhs = image[...].reshape(rows * cols, ch)
            val = taps(lhs, rows, r.wd.at[need.index((k, i))], DILATIONS[k - 1])
            r.part_off[t - 4, step] = val.astype(BF16)

    def second(t):
        core_copy(t).wait_recv()
        for c in range(nx):
            cell = pl.ds(c * cs, cs)
            if t < 4:
                total = r.part_own[t, 1, :, cell].astype(F32) + r.crecv_own[t, :, cell].astype(F32)
                r.xsend_own[t, c] = total.astype(BF16)

                @pl.when(xi == c)
                def _(total=total):
                    r.keep_own[t] = total
            else:
                u = t - 4
                total = r.part_off[u, 1, :, cell].astype(F32) + r.crecv_off[u, :, cell].astype(F32)
                total = jnp.concatenate([total[:1], total[rows - 1 :], total[1 : rows - 1]], axis=0)
                r.xsend_off[u, c] = total.astype(BF16)

                @pl.when(xi == c)
                def _(total=total, u=u):
                    r.keep_off[u] = total

    def sends_to(t):
        k, i, hop = off[t - 4]
        return band + hop < nb if i == 0 else band - hop >= 0

    def gets_from(t):
        k, i, hop = off[t - 4]
        return band - hop >= 0 if i == 0 else band + hop < nb

    def z_copy(t, h):
        k, i, hop = off[t - 4]
        run = pl.ds(*off_cuts[h])
        return rcopy(
            r.zsend.at[t - 4, run], r.zrecv.at[t - 4, run], r.z_s.at[t - 4], r.z_r.at[t - 4, h],
            band=band + hop if i == 0 else band - hop, sect=sect,
        )

    def forward_off(t, h):
        run = pl.ds(*off_cuts[h])
        total = r.keep_off[t - 4, run]
        for e in range(1, nx):
            x_copy(t, h, e, True).wait_recv()
            total = total + r.xrecv_off[t - 4, lax.rem(xi + e, nx), run].astype(F32)
        r.zsend[t - 4, run] = total.astype(BF16)
        z_copy(t, h).start()

    def for_off(fn, *rest):
        for t in range(4, 4 + n_off):
            @pl.when(sends_to(t))
            def _(t=t):
                fn(t, *rest)

    def pool_sect(e, incoming=False):
        other = lax.rem(sect + e, ns)
        slot = other if incoming else sect
        return rcopy(
            r.pool_s.at[sect], r.pool_s.at[slot], r.one_s.at[0], r.one_r.at[0], sect=other
        )

    def pool_band(e, incoming=False):
        other = lax.rem(band + e, nb)
        slot = other if incoming else band
        return rcopy(
            r.pool_b.at[band], r.pool_b.at[slot], r.one_s.at[1], r.one_r.at[1], band=other
        )

    def dot_f32(v, w):
        n = v.shape[0]
        high = v.astype(BF16).astype(F32)
        middle = (v - high).astype(BF16).astype(F32)
        terms = jnp.concatenate([high, middle, v - high - middle], axis=0).astype(BF16)
        p = jnp.dot(terms, w, preferred_element_type=F32)
        return p[:n] + p[n : 2 * n] + p[2 * n :]

    def all_of(ref, n):
        return ref.at[pl.ds(0, n)]

    def arrived(whole, sem):
        pltpu.make_async_copy(whole, whole, sem).wait()

    def pool():
        need_now("wide")
        ones = jnp.ones((8, rows * cols), BF16)
        at = lax.broadcasted_iota(jnp.int32, (8, ch), 0)
        sums = jnp.zeros((8, ch), F32)
        for m, image in ((mine, r.feat_own), (theirs, r.feat.at[0])):
            part = jnp.dot(
                ones, image[...].reshape(rows * cols, ch), preferred_element_type=F32
            )
            sums = jnp.where(at == m, part, sums)
        r.pool_s[sect] = dot_f32(sums, r.wide[0])
        for e in range(1, ns):
            pool_sect(e).start()

    need_now("mask")
    facts = [slots(theirs), slots(mine)]
    on, place_of, row_of = facts[1]

    with scope("w0"):
        need_now("theirs", "first")
    with scope("first0a"):
        first(0, 0)
    with scope("bar"):
        pl.semaphore_wait(bar, (ns - 1) + (nb - 1))
    core_copy(0).start()

    @pl.when(up_ok)
    def _():
        low_up.start()

    @pl.when(dn_ok)
    def _():
        low_dn.start()

    def off_theirs(t):
        first(t, 0)
        core_copy(t).start()

    if n_off:
        need_now("off")
    with scope("offa"):
        for_off(off_theirs)
    need_now("mine")
    with scope("first0b"):
        first(0, 1)
    with scope("pool"):
        pool()
    with scope("second0"):
        second(0)
    for g in range(n_cut):
        send_x(0, g)
    with scope("offb"):
        for_off(first, 1)

    def off_send(t):
        second(t)
        for h in range(2):
            send_x(t, h)

    with scope("offs"):
        for_off(off_send)

    def own_half(t, step):
        with scope(f"first{t}{'ab'[step]}"):
            first(t, step)
        if step == 0:
            core_copy(t).start()

    def own_sum(t):
        with scope(f"second{t}"):
            second(t)
        send_x(t, 0)

    need_now("rest")
    own_half(1, 0)
    own_half(1, 1)
    own_sum(1)
    own_half(2, 0)
    own_half(2, 1)
    own_half(3, 0)
    own_sum(2)
    own_half(3, 1)
    own_sum(3)
    for t in (1, 2):
        for g in range(1, n_cut):
            send_x(t, g)

    with scope("fwd0"):
        for_off(forward_off, 0)

    with scope("low"):
        need_now("low", "wr", "br", "wml", "vec")

        def reduced(v):
            return jax.nn.relu(
                lax.dot_general(
                    v, r.wr[...], (((1,), (1,)), ((), ())), preferred_element_type=F32
                )
                + r.br[...]
            ).astype(BF16)

        r.lowred[1 : rows + 1] = reduced(r.low[...].reshape(rows * cols, low_w)).reshape(
            rows, cols, lowp
        )
        for side, at, ok, copy in ((0, 0, up_ok, low_dn), (1, rows + 1, dn_ok, low_up)):
            @pl.when(ok)
            def _(side=side, at=at, copy=copy):
                copy.wait_recv()
                r.lowred[at] = reduced(r.low_halo[side])

            @pl.when(jnp.logical_not(ok))
            def _(at=at):
                r.lowred[at] = jnp.zeros((cols, lowp), BF16)

    with scope("fwd1"):
        for_off(forward_off, 1)

    with scope("poolb"):
        arrived(all_of(r.pool_s, ns - 1), r.one_r.at[0])
        total = r.pool_s[0]
        for s in range(1, ns):
            total = total + r.pool_s[s]
        r.pool_b[band] = total
    for e in range(1, nb):
        pool_band(e).start()

    def combine(mid, left, right, n):
        r.m_l[:n, pl.ds(pad, cols)] = left.reshape(n, cols, br_w)
        r.m_r[:n, pl.ds(pad, cols)] = right.reshape(n, cols, br_w)
        return (
            mid.reshape(n, cols, br_w)
            + r.m_l[:n, pl.ds(pad - 1, cols)]
            + r.m_r[:n, pl.ds(pad + 1, cols)]
        )

    with scope("lowconv"):
        terms = [None] * 3
        for i in range(3):
            lhs = jnp.concatenate([r.lowred[row_of[p] + i] for p in range(live)], axis=0)
            for j in range(3):
                term = jnp.dot(lhs, r.wml[i, j], preferred_element_type=F32)
                terms[j] = term if i == 0 else terms[j] + term
        r.lowacc[...] = combine(terms[1], terms[0], terms[2], live) + r.vec[0].reshape(1, 1, br_w)

    need_now("wproj", "bbr")
    with scope("ctx"):
        if nb > 1:
            arrived(all_of(r.pool_b, nb - 1), r.one_r.at[1])
        total = r.pool_b[0]
        for b in range(1, nb):
            total = total + r.pool_b[b]
        pooled = jax.nn.relu(total / (nb * rows * cols) + r.vec[1])
        context = dot_f32(pooled, r.wproj[4 * br_w :])
        own = context[0:1]
        for m in range(1, mb):
            own = jnp.where(mine == m, context[m : m + 1], own)
        base = own + r.vec[2]

    def branch(t, g):
        lo, n = cuts[g]
        k = ORDER[t]
        with scope(f"x{t}{g}"):
            if t == 0:
                x_arrived(g)
            if t == 3:
                for e in range(1, nx):
                    x_copy(t, g, e, True).wait_recv()
        for u in range(4, 4 + n_off):
            if off[u - 4][0] == k:
                @pl.when(gets_from(u))
                def _(u=u):
                    with scope(f"z{g}"):
                        if g < 2:
                            z_copy(u, g).wait_recv()
                    for p in range(lo, lo + n):
                        at = p if p < 2 else row_of[p] + 1
                        r.keep_own[t, p] = r.keep_own[t, p] + r.zrecv[u - 4, at].astype(F32)
        total = r.keep_own[t, lo : lo + n]
        for e in range(1, nx):
            total = total + r.xrecv_own[t, lax.rem(xi + e, nx), lo : lo + n].astype(F32)
        total = jax.nn.relu(total + r.bbr[k : k + 1].reshape(1, 1, br_w)).astype(BF16)
        return jnp.dot(
            total.reshape(n * cs, br_w), r.wproj[k * br_w : (k + 1) * br_w],
            preferred_element_type=F32,
        )

    def gather_x(g, e, incoming=False):
        run = pl.ds(*cuts[g])
        other = lax.rem(xi + e, nx)
        slot = other if incoming else xi
        return rcopy(
            r.gath.at[xi, run], r.gath.at[slot, run],
            r.one_s.at[2], r.gx_r.at[g, (e if incoming else nx - e) - 1], sect=other * 2 + core,
        )

    def early(g):
        lo, n = cuts[g]
        acc = branch(0, g)
        for t in (1, 2):
            acc = acc + branch(t, g)
        r.acc[lo : lo + n] = (acc + base).reshape(n, cs, br_w)

    def project(g):
        lo, n = cuts[g]
        last = branch(3, g).reshape(n, cs, br_w)
        done = jax.nn.relu(r.acc[lo : lo + n] + last)
        for p in range(n):
            v = done[p]
            if lo + p < 2:
                v = v * on[(0, rows - 1)[lo + p]].astype(F32)
            r.gath[xi, lo + p] = v.astype(BF16)
        for e in range(1, nx):
            gather_x(g, e).start()

    def halo_copy(side, c):
        return rcopy(
            r.gath.at[c, 1 - side], r.halo.at[side, c], r.h_s.at[side], r.h_r.at[side],
            band=band + 1 if side == 0 else band - 1, sect=sect,
        )

    early(0)
    project(0)
    for g in range(1, n_cut):
        send_x(3, g)
    for g in range(1, n_cut):
        early(g)
    with scope("ga"):
        for e in range(1, nx):
            gather_x(0, e, True).wait_recv()
    for side, ok in ((0, dn_ok), (1, up_ok)):
        @pl.when(ok)
        def _(side=side):
            for c in range(nx):
                halo_copy(side, c).start()
    for p, y in ((0, 0), (1, rows - 1)):
        for c in range(nx):
            r.joined[y + 1, pl.ds(c * cs, cs)] = r.gath[c, p]
    for g in range(1, n_cut):
        project(g)
    need_now("wmp")
    for side, at, ok in ((0, 0, up_ok), (1, rows + 1, dn_ok)):
        @pl.when(ok)
        def _(side=side, at=at):
            with scope("hw"):
                arrived(r.halo.at[side], r.h_r.at[side])
            for c in range(nx):
                r.joined[at, pl.ds(c * cs, cs)] = r.halo[side, c]
    with scope("gb"):
        for g in range(1, n_cut):
            for e in range(1, nx):
                gather_x(g, e, True).wait_recv()
    with scope("join"):
        for y in range(1, rows - 1):
            for c in range(nx):
                r.joined[y + 1, pl.ds(c * cs, cs)] = (
                    r.gath[c, place_of[y]].astype(F32) * on[y].astype(F32)
                ).astype(BF16)

    def merged_copy(h):
        run = pl.ds(*halves[h])
        return rcopy(
            r.merged.at[run], r.merged_in.at[run], r.one_s.at[3], r.one_r.at[2], sect=peer
        )

    halves = [(0, 2), (2, live - 2)]
    for h, (lo, n) in enumerate(halves):
        with scope(f"merge{h}"):
            lhs = jnp.concatenate(
                [
                    jnp.concatenate([r.joined[row_of[p] + i] for p in range(lo, lo + n)], axis=0)
                    for i in range(3)
                ],
                axis=1,
            )
            left, mid, right = [
                jnp.dot(lhs, r.wmp[j], preferred_element_type=F32) for j in range(3)
            ]
            total = combine(mid, left, right, n) + r.lowacc[lo : lo + n]
            r.merged[lo : lo + n] = jax.nn.relu(total).astype(BF16)
        merged_copy(h).start()

    def spread(image, src, flags, places):
        for y in range(rows):
            r.out[image, y] = (src[places[y]].astype(F32) * flags[y].astype(F32)).astype(BF16)

    with scope("spread"):
        spread(mine, r.merged, on, place_of)
    with scope("ow"):
        arrived(r.merged, r.one_r.at[2])
    with scope("spread2"):
        spread(theirs, r.merged_in, facts[0][0], facts[0][1])

    @pl.when(up_ok)
    def _():
        low_up.wait_send()

    @pl.when(dn_ok)
    def _():
        low_dn.wait_send()

    def off_sent(t):
        u = t - 4
        core_copy(t).wait_send()
        if nx > 1:
            arrived(all_of(r.xsend_off.at[u], nx - 1), r.x_s.at[1 + u])
        arrived(r.zsend.at[u], r.z_s.at[u])

    for_off(off_sent)
    arrived(r.part_own.at[:, 0], r.c_s.at[0])
    if nx > 1:
        arrived(r.xsend_own.at[:, pl.ds(0, nx - 1)], r.x_s.at[0])
        arrived(all_of(r.gath, nx - 1), r.one_s.at[2])
    arrived(all_of(r.pool_s, ns - 1), r.one_s.at[0])
    if nb > 1:
        arrived(all_of(r.pool_b, nb - 1), r.one_s.at[1])
    for side, ok in ((0, dn_ok), (1, up_ok)):
        @pl.when(ok)
        def _(side=side):
            arrived(r.halo.at[side], r.h_s.at[side])
    arrived(r.merged, r.one_s.at[3])


def shards(
    features, low_level, land_mask, weight_one, weight_dilated, bias_branch, weight_pool,
    bias_pool, weight_project, bias_project, weight_reduce, bias_reduce, weight_merging,
    bias_merging,
):
    mb, rows, cols, ch = features.shape
    br_w = weight_project.shape[1]
    dec = weight_merging.shape[3]
    low_w, lowp = weight_reduce.shape
    nb, ns = lax.axis_size("band"), lax.axis_size("sect")
    nx = ns // 2
    cs = cols // nx
    assert mb == 2 and ns % 2 == 0 and rows > 2
    live = rows // LAND_BLOCK * LAND_MOST if rows % LAND_BLOCK == 0 else rows
    off = offsets(rows, nb)
    n_off = max(len(off), 1)
    assert dec == br_w
    n_cut = len(pieces(live))
    pad = -(-max(DILATIONS) // 8) * 8
    vm, dma = pltpu.VMEM, pltpu.SemaphoreType.DMA
    dims = (mb, rows, cols, ch, br_w, live, nb, ns, low_w, lowp)
    args = dict(
        mask_h=land_mask, feat_h=features, low_h=low_level, w1_h=weight_one, wd_h=weight_dilated,
        bbr_h=bias_branch, wpool_h=weight_pool, bpool_h=bias_pool.reshape(1, -1),
        wproj_h=weight_project, bproj_h=bias_project.reshape(1, -1), wr_h=weight_reduce.T,
        br_h=bias_reduce.reshape(1, -1), wm_h=weight_merging, bm_h=bias_merging.reshape(1, -1),
    )
    scratch = dict(
        mask=pltpu.SMEM(land_mask.shape, jnp.int32),
        feat=vm((1, rows, cols, ch), BF16),
        feat_own=vm((rows, cols, ch), BF16),
        low=vm((rows, cols, low_w), BF16),
        low_halo=vm((2, cols, low_w), BF16),
        wide=vm((2, ch, br_w), BF16),
        wd=vm((3 + len(off), 3, ch, br_w), BF16),
        wproj=vm(weight_project.shape, BF16),
        wmp=vm((3, 3 * br_w, dec), BF16),
        wml=vm((3, 3, lowp, dec), BF16),
        wr=vm((lowp, low_w), BF16),
        br=vm((1, lowp), F32),
        vec=vm((3, 1, br_w), F32),
        bbr=vm(bias_branch.shape, F32),
        m_l=vm((rows, cols + 2 * pad, br_w), F32),
        m_r=vm((rows, cols + 2 * pad, br_w), F32),
        part_off=vm((n_off, 2, rows, cols, br_w), BF16),
        crecv_off=vm((n_off, rows, cols, br_w), BF16),
        xsend_off=vm((n_off, nx, rows, cs, br_w), BF16),
        xrecv_off=vm((n_off, nx, rows, cs, br_w), BF16),
        zsend=vm((n_off, rows, cs, br_w), BF16),
        zrecv=vm((n_off, rows, cs, br_w), BF16),
        keep_off=vm((n_off, rows, cs, br_w), F32),
        part_own=vm((4, 2, live, cols, br_w), BF16),
        crecv_own=vm((4, live, cols, br_w), BF16),
        xsend_own=vm((4, nx, live, cs, br_w), BF16),
        xrecv_own=vm((4, nx, live, cs, br_w), BF16),
        keep_own=vm((4, live, cs, br_w), F32),
        acc=vm((live, cs, br_w), F32),
        pool_s=vm((ns, 8, br_w), F32),
        pool_b=vm((nb, 8, br_w), F32),
        gath=vm((nx, live, cs, br_w), BF16),
        halo=vm((2, nx, cs, br_w), BF16),
        joined=vm((rows + 2, cols, br_w), BF16),
        lowred=vm((rows + 2, cols, lowp), BF16),
        lowacc=vm((live, cols, dec), F32),
        merged=vm((live, cols, dec), BF16),
        merged_in=vm((live, cols, dec), BF16),
        loc_sem=dma((15,)),
        one_s=dma((4,)),
        one_r=dma((3,)),
        lo_s=dma((2,)),
        lo_r=dma((2,)),
        c_s=dma((1 + n_off,)),
        c_r=dma((4 + n_off,)),
        x_s=dma((1 + n_off,)),
        x_r=dma((2 * n_cut + 2 * n_off, max(nx - 1, 1))),
        z_s=dma((n_off,)),
        z_r=dma((n_off, 2)),
        gx_r=dma((n_cut, max(nx - 1, 1))),
        h_s=dma((2,)),
        h_r=dma((2,)),
    )
    names = (*args, "out", *scratch)
    merged_map = pl.pallas_call(
        functools.partial(kernel, dims, names),
        out_shape=jax.ShapeDtypeStruct((mb, rows, cols, dec), BF16),
        in_specs=[pl.BlockSpec(memory_space=pltpu.HBM)] * len(args),
        out_specs=pl.BlockSpec(memory_space=pltpu.VMEM),
        scratch_shapes=list(scratch.values()),
        compiler_params=pltpu.CompilerParams(
            collective_id=0, has_side_effects=True, vmem_limit_bytes=48 * 1024 * 1024
        ),
    )(*[pltpu.with_memory_space_constraint(a, pltpu.HBM) for a in args.values()])
    return jnp.maximum(merged_map, jnp.zeros_like(merged_map))


def solution(mesh):
    in_specs = (
        P("grp", "band", None, "sect"),
        P("grp", "band", None, None),
        P("grp", "band"),
        P("sect", None),
        P(None, None, None, "sect", None),
        P(),
        P("sect", None),
        P(),
        P(),
        P(),
        P(),
        P(),
        P(),
        P(),
    )
    out_specs = P("grp", "band", None, None)
    return jax.shard_map(shards, mesh=mesh, in_specs=in_specs, out_specs=out_specs, check_vma=False)
```

time: 33.2 us -> 32.3 us (0.973)
  other arithmetic: 2.67 us -> 0.85 us
  Pallas kernels: 30.3 us -> 31.3 us
    select_n x1 -> x0, other arithmetic: 1.99 us -> none  [shards(): jnp.where(land_mask[:, :, None, None] != 0, merged_map, jnp.zeros_like(me...]
    pallas_call x1, Pallas kernels: 30.3 us -> 31.3 us  [shards(): pl.pallas_call(functools.partial(kernel, dims, names), out_shape=jax.Shap...]
    max x0 -> x1, other arithmetic: none -> 0.85 us  [shards(): return jnp.maximum(merged_map, jnp.zeros_like(merged_map))]
    ne x1 -> x0, other arithmetic: 0.68 us -> none  [shards(): land_mask[:, :, None, None] != 0]
where the time goes in v1:
time: 32.3 us; the launch traced here: 32.1 us
  Pallas kernels  31.3 us (97%)
  other arithmetic  0.85 us (3%)
    pallas_call x1, Pallas kernels, shards(): pl.pallas_call(functools.partial(kernel, dims, names), out_shape=jax.Shap...  31.3 us
    max x1, other arithmetic, shards(): return jnp.maximum(merged_map, jnp.zeros_like(merged_map))  0.85 us

profile of v1, /device:TPU:0, one launch (start us, length us, event | category | flops | bytes accessed | tf_op | source)
XLA Modules:
  0.0 32.1 jit_solution(15990243831763159468)
XLA Ops:
  0.0 31.3 %shard_map.136 = bf16[2,6,96,256]{3,2,1,0:T(8,128)(2,1)S(1)} custom-call(s32[2,6]{1,0:T(2,128)} %refs_0_.1, bf16[2,6,96,512]{3,2,1,0:T(8,128)(2,1)} %refs_1_.1, bf16[2,6,96,256]{3,2,1,0:T(8,128)(2,1)} %refs_2_.1, bf16[512,256]{1,0:T(8,128)(2,1)} %refs_3_.1, bf16[3,3,3,512,256]{4,3,2,1,0:T(8,128)(2,1)} %refs_4_.1, f32[4,256]{1,0:T(4,128)} %refs_5_.1, ...), custom_call_target="tpu_custom_call" | custom-call | tf_op jit(solution)/shard_map/pallas_call | solution.py:696
  31.3 0.9 %broadcast_maximum_fusion = bf16[2,6,96,256]{3,2,1,0:T(8,128)(2,1)} fusion(bf16[2,6,96,256]{3,2,1,0:T(8,128)(2,1)S(1)} %shard_map.136), kind=kLoop, calls=%fused_computation | loop fusion | flops 294912 | bytes 1179648 | tf_op jit(solution)/shard_map/max | solution.py:706

commit v2 on v1

--- a/solution.py
+++ b/solution.py
@@ -14,7 +14,7 @@
 MESH = pl.DeviceIdType.MESH
 F32 = jnp.float32
 BF16 = jnp.bfloat16
-ORDER = (3, 2, 0, 1)
+ORDER = (0, 3, 2, 1)
 
 
 def offsets(rows, bands):
@@ -48,7 +48,7 @@
     n_off = len(off)
     cuts = pieces(live)
     n_cut = len(cuts)
-    off_cuts = [(0, 2), (2, rows - 2)]
+    off_cuts = [(0, 2), (2, live - 2)]
     need = [(k, 1) for k in ORDER if k] + [(k, i) for k, i, _ in off]
     pad = (r.m_l.shape[1] - cols) // 2
     scope = jax.named_scope
@@ -77,14 +77,13 @@
 
     fetch("mask", (r.mask_h, r.mask), whole=r.mask)
     fetch("theirs", (r.feat_h.at[theirs], r.feat.at[0]), whole=r.feat.at[0])
-    fetch("first", taps_of(*need[0]), whole=r.wd.at[0])
+    fetch("w1", (r.w1_h, r.w1), whole=r.w1)
     fetch("mine", (r.feat_h.at[mine], r.feat_own), whole=r.feat_own)
-    fetch(
-        "wide", (r.wpool_h, r.wide.at[0]), (r.w1_h, r.wide.at[1]), whole=r.wide
-    )
+    fetch("wpool", (r.wpool_h, r.wpool), whole=r.wpool)
     if n_off:
         fetch("off", *[taps_of(*n) for n in need[3:]], whole=r.wd.at[pl.ds(3, n_off)])
-    fetch("rest", *[taps_of(*n) for n in need[1:3]], whole=r.wd.at[pl.ds(1, 2)])
+    fetch("taps0", taps_of(*need[0]), whole=r.wd.at[0])
+    fetch("taps1", *[taps_of(*n) for n in need[1:3]], whole=r.wd.at[pl.ds(1, 2)])
     fetch("low", (r.low_h.at[mine], r.low), whole=r.low)
     fetch("wr", (r.wr_h, r.wr), whole=r.wr)
     fetch("br", (r.br_h, r.br), whole=r.br)
@@ -133,14 +132,16 @@
         on = [r.mask[m, y] for y in range(rows)]
         place_of = [0] + [None] * (rows - 2) + [1]
         row_of = [0, rows - 1] + [jnp.int32(0)] * (live - 2)
+        hits = {}
         count = jnp.int32(0)
         for y in range(1, rows - 1):
             place_of[y] = jnp.where(on[y] > 0, jnp.minimum(count + 2, live - 1), 0)
             for p in range(2, live):
                 hit = jnp.logical_and(on[y] > 0, count == p - 2)
                 row_of[p] = jnp.where(hit, y, row_of[p])
+                hits[p, y] = jnp.where(hit, 1, 0)
             count = count + on[y]
-        return on, place_of, row_of
+        return on, place_of, row_of, hits
 
     for ref in (r.m_l, r.m_r):
         zero = jnp.zeros((ref.shape[0], pad, br_w), F32)
@@ -201,7 +202,7 @@
             if k:
                 val = taps(lhs, live, r.wd.at[need.index((k, 1))], DILATIONS[k - 1])
             else:
-                val = jnp.dot(lhs, r.wide[1], preferred_element_type=F32).reshape(live, cols, br_w)
+                val = jnp.dot(lhs, r.w1[...], preferred_element_type=F32).reshape(live, cols, br_w)
             r.part_own[t, step] = val.astype(BF16)
         else:
             k, i, _ = off[t - 4]
@@ -213,22 +214,44 @@
         core_copy(t).wait_recv()
         for c in range(nx):
             cell = pl.ds(c * cs, cs)
-            if t < 4:
-                total = r.part_own[t, 1, :, cell].astype(F32) + r.crecv_own[t, :, cell].astype(F32)
-                r.xsend_own[t, c] = total.astype(BF16)
-
-                @pl.when(xi == c)
-                def _(total=total):
-                    r.keep_own[t] = total
+            total = r.part_own[t, 1, :, cell].astype(F32) + r.crecv_own[t, :, cell].astype(F32)
+            r.xsend_own[t, c] = total.astype(BF16)
+
+            @pl.when(xi == c)
+            def _(total=total):
+                r.keep_own[t] = total
+
+    def second_off(t, h):
+        u = t - 4
+        if h == 0:
+            core_copy(t).wait_recv()
+        else:
+            sel_copy(t).wait_recv()
+        lo, n = off_cuts[h]
+        for c in range(nx):
+            cell = pl.ds(c * cs, cs)
+
+            def row(y, cell=cell):
+                return r.part_off[u, 1, y, cell].astype(F32) + r.crecv_off[u, y, cell].astype(F32)
+
+            if h == 0:
+                picked = [row(0), row(rows - 1)]
             else:
-                u = t - 4
-                total = r.part_off[u, 1, :, cell].astype(F32) + r.crecv_off[u, :, cell].astype(F32)
-                total = jnp.concatenate([total[:1], total[rows - 1 :], total[1 : rows - 1]], axis=0)
-                r.xsend_off[u, c] = total.astype(BF16)
-
-                @pl.when(xi == c)
-                def _(total=total, u=u):
-                    r.keep_off[u] = total
+                inner = [row(y) for y in range(1, rows - 1)]
+                picked = []
+                for p in range(2, live):
+                    total = jnp.zeros((cs, br_w), F32)
+                    for y in range(1, rows - 1):
+                        at = (p - 2) * (rows - 2) + y - 1
+                        total = total + inner[y - 1] * r.sel_in[u, at : at + 1]
+                    picked.append(total)
+            for p, total in enumerate(picked):
+                r.xsend_off[u, c, lo + p] = total.astype(BF16)
+
+            @pl.when(xi == c)
+            def _(picked=picked):
+                for p, total in enumerate(picked):
+                    r.keep_off[u, lo + p] = total
 
     def sends_to(t):
         k, i, hop = off[t - 4]
@@ -237,6 +260,13 @@
     def gets_from(t):
         k, i, hop = off[t - 4]
         return band - hop >= 0 if i == 0 else band + hop < nb
+
+    def sel_copy(t):
+        k, i, hop = off[t - 4]
+        return rcopy(
+            r.sel_out, r.sel_in.at[t - 4], r.s_s.at[t - 4], r.s_r.at[t - 4],
+            band=band - hop if i == 0 else band + hop, sect=sect,
+        )
 
     def z_copy(t, h):
         k, i, hop = off[t - 4]
@@ -290,7 +320,7 @@
         pltpu.make_async_copy(whole, whole, sem).wait()
 
     def pool():
-        need_now("wide")
+        need_now("wpool")
         ones = jnp.ones((8, rows * cols), BF16)
         at = lax.broadcasted_iota(jnp.int32, (8, ch), 0)
         sums = jnp.zeros((8, ch), F32)
@@ -299,21 +329,44 @@
                 ones, image[...].reshape(rows * cols, ch), preferred_element_type=F32
             )
             sums = jnp.where(at == m, part, sums)
-        r.pool_s[sect] = dot_f32(sums, r.wide[0])
+        r.pool_s[sect] = dot_f32(sums, r.wpool[...])[:mb]
         for e in range(1, ns):
             pool_sect(e).start()
 
     need_now("mask")
     facts = [slots(theirs), slots(mine)]
-    on, place_of, row_of = facts[1]
+    on, place_of, row_of, hits = facts[1]
+
+    for p in range(2, live):
+        for y in range(1, rows - 1):
+            at = (p - 2) * (rows - 2) + y - 1
+            r.sel_out[at : at + 1] = jnp.full((1, br_w), hits[p, y].astype(F32))
+
+    def own_half(t, step):
+        with scope(f"first{t}{'ab'[step]}"):
+            first(t, step)
+        if step == 0:
+            core_copy(t).start()
+
+    def off_theirs(t):
+        first(t, 0)
+        core_copy(t).start()
+
+    def off_send(t, h):
+        second_off(t, h)
+        send_x(t, h)
 
     with scope("w0"):
-        need_now("theirs", "first")
+        need_now("theirs", "w1")
     with scope("first0a"):
         first(0, 0)
     with scope("bar"):
         pl.semaphore_wait(bar, (ns - 1) + (nb - 1))
     core_copy(0).start()
+    for t in range(4, 4 + n_off):
+        @pl.when(gets_from(t))
+        def _(t=t):
+            sel_copy(t).start()
 
     @pl.when(up_ok)
     def _():
@@ -323,89 +376,37 @@
     def _():
         low_dn.start()
 
-    def off_theirs(t):
-        first(t, 0)
-        core_copy(t).start()
-
+    need_now("mine")
+    own_half(0, 1)
+    with scope("pool"):
+        pool()
     if n_off:
         need_now("off")
     with scope("offa"):
         for_off(off_theirs)
-    need_now("mine")
-    with scope("first0b"):
-        first(0, 1)
-    with scope("pool"):
-        pool()
     with scope("second0"):
         second(0)
     for g in range(n_cut):
         send_x(0, g)
     with scope("offb"):
         for_off(first, 1)
-
-    def off_send(t):
-        second(t)
-        for h in range(2):
-            send_x(t, h)
-
-    with scope("offs"):
-        for_off(off_send)
-
-    def own_half(t, step):
-        with scope(f"first{t}{'ab'[step]}"):
-            first(t, step)
-        if step == 0:
-            core_copy(t).start()
-
-    def own_sum(t):
-        with scope(f"second{t}"):
-            second(t)
-        send_x(t, 0)
-
-    need_now("rest")
+    with scope("offs0"):
+        for_off(off_send, 0)
+    need_now("taps0")
     own_half(1, 0)
     own_half(1, 1)
-    own_sum(1)
+    with scope("second1"):
+        second(1)
+    send_x(1, 0)
+    with scope("offs1"):
+        for_off(off_send, 1)
+    need_now("taps1")
     own_half(2, 0)
     own_half(2, 1)
     own_half(3, 0)
-    own_sum(2)
-    own_half(3, 1)
-    own_sum(3)
-    for t in (1, 2):
-        for g in range(1, n_cut):
-            send_x(t, g)
-
-    with scope("fwd0"):
-        for_off(forward_off, 0)
-
-    with scope("low"):
-        need_now("low", "wr", "br", "wml", "vec")
-
-        def reduced(v):
-            return jax.nn.relu(
-                lax.dot_general(
-                    v, r.wr[...], (((1,), (1,)), ((), ())), preferred_element_type=F32
-                )
-                + r.br[...]
-            ).astype(BF16)
-
-        r.lowred[1 : rows + 1] = reduced(r.low[...].reshape(rows * cols, low_w)).reshape(
-            rows, cols, lowp
-        )
-        for side, at, ok, copy in ((0, 0, up_ok, low_dn), (1, rows + 1, dn_ok, low_up)):
-            @pl.when(ok)
-            def _(side=side, at=at, copy=copy):
-                copy.wait_recv()
-                r.lowred[at] = reduced(r.low_halo[side])
-
-            @pl.when(jnp.logical_not(ok))
-            def _(at=at):
-                r.lowred[at] = jnp.zeros((cols, lowp), BF16)
-
-    with scope("fwd1"):
-        for_off(forward_off, 1)
-
+    with scope("second2"):
+        second(2)
+    send_x(2, 0)
     with scope("poolb"):
         arrived(all_of(r.pool_s, ns - 1), r.one_r.at[0])
         total = r.pool_s[0]
@@ -414,6 +415,43 @@
         r.pool_b[band] = total
     for e in range(1, nb):
         pool_band(e).start()
+    own_half(3, 1)
+    with scope("second3"):
+        second(3)
+    send_x(3, 0)
+    for t in (1, 2):
+        for g in range(1, n_cut):
+            send_x(t, g)
+
+    with scope("fwd0"):
+        for_off(forward_off, 0)
+
+    with scope("low"):
+        need_now("low", "wr", "br", "wml", "vec")
+
+        def reduced(v):
+            return jax.nn.relu(
+                lax.dot_general(
+                    v, r.wr[...], (((1,), (1,)), ((), ())), preferred_element_type=F32
+                )
+                + r.br[...]
+            ).astype(BF16)
+
+        r.lowred[1 : rows + 1] = reduced(r.low[...].reshape(rows * cols, low_w)).reshape(
+            rows, cols, lowp
+        )
+        for side, at, ok, copy in ((0, 0, up_ok, low_dn), (1, rows + 1, dn_ok, low_up)):
+            @pl.when(ok)
+            def _(side=side, at=at, copy=copy):
+                copy.wait_recv()
+                r.lowred[at] = reduced(r.low_halo[side])
+
+            @pl.when(jnp.logical_not(ok))
+            def _(at=at):
+                r.lowred[at] = jnp.zeros((cols, lowp), BF16)
+
+    with scope("fwd1"):
+        for_off(forward_off, 1)
 
     def combine(mid, left, right, n):
         r.m_l[:n, pl.ds(pad, cols)] = left.reshape(n, cols, br_w)
@@ -463,9 +501,8 @@
                     with scope(f"z{g}"):
                         if g < 2:
                             z_copy(u, g).wait_recv()
-                    for p in range(lo, lo + n):
-                        at = p if p < 2 else row_of[p] + 1
-                        r.keep_own[t, p] = r.keep_own[t, p] + r.zrecv[u - 4, at].astype(F32)
+                    run = pl.ds(lo, n)
+                    r.keep_own[t, run] = r.keep_own[t, run] + r.zrecv[u - 4, run].astype(F32)
         total = r.keep_own[t, lo : lo + n]
         for e in range(1, nx):
             total = total + r.xrecv_own[t, lax.rem(xi + e, nx), lo : lo + n].astype(F32)
@@ -596,6 +633,10 @@
             arrived(all_of(r.xsend_off.at[u], nx - 1), r.x_s.at[1 + u])
         arrived(r.zsend.at[u], r.z_s.at[u])
 
+    for t in range(4, 4 + n_off):
+        @pl.when(gets_from(t))
+        def _(t=t):
+            sel_copy(t).wait_send()
     for_off(off_sent)
     arrived(r.part_own.at[:, 0], r.c_s.at[0])
     if nx > 1:
@@ -629,6 +670,7 @@
     n_off = max(len(off), 1)
     assert dec == br_w
     n_cut = len(pieces(live))
+    n_sel = -(-(live - 2) * (rows - 2) // 8) * 8
     pad = -(-max(DILATIONS) // 8) * 8
     vm, dma = pltpu.VMEM, pltpu.SemaphoreType.DMA
     dims = (mb, rows, cols, ch, br_w, live, nb, ns, low_w, lowp)
@@ -644,7 +686,10 @@
         feat_own=vm((rows, cols, ch), BF16),
         low=vm((rows, cols, low_w), BF16),
         low_halo=vm((2, cols, low_w), BF16),
-        wide=vm((2, ch, br_w), BF16),
+        w1=vm(weight_one.shape, BF16),
+        wpool=vm(weight_pool.shape, BF16),
+        sel_out=vm((n_sel, br_w), F32),
+        sel_in=vm((n_off, n_sel, br_w), F32),
         wd=vm((3 + len(off), 3, ch, br_w), BF16),
         wproj=vm(weight_project.shape, BF16),
         wmp=vm((3, 3 * br_w, dec), BF16),
@@ -657,19 +702,19 @@
         m_r=vm((rows, cols + 2 * pad, br_w), F32),
         part_off=vm((n_off, 2, rows, cols, br_w), BF16),
         crecv_off=vm((n_off, rows, cols, br_w), BF16),
-        xsend_off=vm((n_off, nx, rows, cs, br_w), BF16),
-        xrecv_off=vm((n_off, nx, rows, cs, br_w), BF16),
-        zsend=vm((n_off, rows, cs, br_w), BF16),
-        zrecv=vm((n_off, rows, cs, br_w), BF16),
-        keep_off=vm((n_off, rows, cs, br_w), F32),
+        xsend_off=vm((n_off, nx, live, cs, br_w), BF16),
+        xrecv_off=vm((n_off, nx, live, cs, br_w), BF16),
+        zsend=vm((n_off, live, cs, br_w), BF16),
+        zrecv=vm((n_off, live, cs, br_w), BF16),
+        keep_off=vm((n_off, live, cs, br_w), F32),
         part_own=vm((4, 2, live, cols, br_w), BF16),
         crecv_own=vm((4, live, cols, br_w), BF16),
         xsend_own=vm((4, nx, live, cs, br_w), BF16),
         xrecv_own=vm((4, nx, live, cs, br_w), BF16),
         keep_own=vm((4, live, cs, br_w), F32),
         acc=vm((live, cs, br_w), F32),
-        pool_s=vm((ns, 8, br_w), F32),
-        pool_b=vm((nb, 8, br_w), F32),
+        pool_s=vm((ns, mb, br_w), F32),
+        pool_b=vm((nb, mb, br_w), F32),
         gath=vm((nx, live, cs, br_w), BF16),
         halo=vm((2, nx, cs, br_w), BF16),
         joined=vm((rows + 2, cols, br_w), BF16),
@@ -677,7 +722,7 @@
         lowacc=vm((live, cols, dec), F32),
         merged=vm((live, cols, dec), BF16),
         merged_in=vm((live, cols, dec), BF16),
-        loc_sem=dma((15,)),
+        loc_sem=dma((16,)),
         one_s=dma((4,)),
         one_r=dma((3,)),
         lo_s=dma((2,)),
@@ -686,6 +731,8 @@
         c_r=dma((4 + n_off,)),
         x_s=dma((1 + n_off,)),
         x_r=dma((2 * n_cut + 2 * n_off, max(nx - 1, 1))),
+        s_s=dma((n_off,)),
+        s_r=dma((n_off,)),
         z_s=dma((n_off,)),
         z_r=dma((n_off, 2)),
         gx_r=dma((n_cut, max(nx - 1, 1))),

time: 32.3 us -> 27.9 us (0.86); the launches traced: 32.1 us -> 27.3 us
  Pallas kernels: 31.3 us -> 26.5 us
    pallas_call x1, Pallas kernels: 31.3 us -> 26.5 us  [shards(): pl.pallas_call(functools.partial(kernel, dims, names), out_shape=jax.Shap...]
where the time goes in v2:
time: 27.9 us; the launch traced here: 27.3 us
  Pallas kernels  26.5 us (95%)
  other arithmetic  0.85 us (3%)
    pallas_call x1, Pallas kernels, shards(): pl.pallas_call(functools.partial(kernel, dims, names), out_shape=jax.Shap...  26.5 us
    max x1, other arithmetic, shards(): return jnp.maximum(merged_map, jnp.zeros_like(merged_map))  0.85 us

profile of v2, /device:TPU:0, one launch (start us, length us, event | category | flops | bytes accessed | tf_op | source)
XLA Modules:
  0.0 27.3 jit_solution(14569280467755425992)
XLA Ops:
  0.0 26.5 %shard_map.136 = bf16[2,6,96,256]{3,2,1,0:T(8,128)(2,1)S(1)} custom-call(s32[2,6]{1,0:T(2,128)} %refs_0_.1, bf16[2,6,96,512]{3,2,1,0:T(8,128)(2,1)} %refs_1_.1, bf16[2,6,96,256]{3,2,1,0:T(8,128)(2,1)} %refs_2_.1, bf16[512,256]{1,0:T(8,128)(2,1)} %refs_3_.1, bf16[3,3,3,512,256]{4,3,2,1,0:T(8,128)(2,1)} %refs_4_.1, f32[4,256]{1,0:T(4,128)} %refs_5_.1, ...), custom_call_target="tpu_custom_call" | custom-call | tf_op jit(solution)/shard_map/pallas_call | solution.py:743
  26.5 0.9 %broadcast_maximum_fusion = bf16[2,6,96,256]{3,2,1,0:T(8,128)(2,1)} fusion(bf16[2,6,96,256]{3,2,1,0:T(8,128)(2,1)S(1)} %shard_map.136), kind=kLoop, calls=%fused_computation | loop fusion | flops 294912 | bytes 1179648 | tf_op jit(solution)/shard_map/max | solution.py:753

commit v3 on v2

--- a/solution.py
+++ b/solution.py
@@ -380,14 +380,14 @@
     own_half(0, 1)
     with scope("pool"):
         pool()
+    with scope("second0"):
+        second(0)
+    for g in range(n_cut):
+        send_x(0, g)
     if n_off:
         need_now("off")
     with scope("offa"):
         for_off(off_theirs)
-    with scope("second0"):
-        second(0)
-    for g in range(n_cut):
-        send_x(0, g)
     with scope("offb"):
         for_off(first, 1)
     with scope("offs0"):
@@ -395,18 +395,6 @@
     need_now("taps0")
     own_half(1, 0)
     own_half(1, 1)
-    with scope("second1"):
-        second(1)
-    send_x(1, 0)
-    with scope("offs1"):
-        for_off(off_send, 1)
-    need_now("taps1")
-    own_half(2, 0)
-    own_half(2, 1)
-    own_half(3, 0)
-    with scope("second2"):
-        second(2)
-    send_x(2, 0)
     with scope("poolb"):
         arrived(all_of(r.pool_s, ns - 1), r.one_r.at[0])
         total = r.pool_s[0]
@@ -415,16 +403,29 @@
         r.pool_b[band] = total
     for e in range(1, nb):
         pool_band(e).start()
+    with scope("second1"):
+        second(1)
+    send_x(1, 0)
+    with scope("offs1"):
+        for_off(off_send, 1)
+    for g in range(1, n_cut):
+        send_x(1, g)
+    need_now("taps1")
+    own_half(2, 0)
+    own_half(2, 1)
+    own_half(3, 0)
+    with scope("second2"):
+        second(2)
+    send_x(2, 0)
+    with scope("fwd0"):
+        for_off(forward_off, 0)
     own_half(3, 1)
     with scope("second3"):
         second(3)
     send_x(3, 0)
-    for t in (1, 2):
+    for t in (2, 3):
         for g in range(1, n_cut):
             send_x(t, g)
-
-    with scope("fwd0"):
-        for_off(forward_off, 0)
 
     with scope("low"):
         need_now("low", "wr", "br", "wml", "vec")
@@ -449,9 +450,6 @@
             @pl.when(jnp.logical_not(ok))
             def _(at=at):
                 r.lowred[at] = jnp.zeros((cols, lowp), BF16)
-
-    with scope("fwd1"):
-        for_off(forward_off, 1)
 
     def combine(mid, left, right, n):
         r.m_l[:n, pl.ds(pad, cols)] = left.reshape(n, cols, br_w)
@@ -470,6 +468,9 @@
                 term = jnp.dot(lhs, r.wml[i, j], preferred_element_type=F32)
                 terms[j] = term if i == 0 else terms[j] + term
         r.lowacc[...] = combine(terms[1], terms[0], terms[2], live) + r.vec[0].reshape(1, 1, br_w)
+
+    with scope("fwd1"):
+        for_off(forward_off, 1)
 
     need_now("wproj", "bbr")
     with scope("ctx"):
@@ -546,33 +547,27 @@
             band=band + 1 if side == 0 else band - 1, sect=sect,
         )
 
+    def send_halo(c):
+        for side, ok in ((0, dn_ok), (1, up_ok)):
+            @pl.when(ok)
+            def _(side=side):
+                halo_copy(side, c).start()
+
     early(0)
     project(0)
-    for g in range(1, n_cut):
-        send_x(3, g)
+    send_halo(xi)
     for g in range(1, n_cut):
         early(g)
-    with scope("ga"):
-        for e in range(1, nx):
-            gather_x(0, e, True).wait_recv()
-    for side, ok in ((0, dn_ok), (1, up_ok)):
-        @pl.when(ok)
-        def _(side=side):
-            for c in range(nx):
-                halo_copy(side, c).start()
-    for p, y in ((0, 0), (1, rows - 1)):
-        for c in range(nx):
-            r.joined[y + 1, pl.ds(c * cs, cs)] = r.gath[c, p]
     for g in range(1, n_cut):
         project(g)
+    for e in range(1, nx):
+        with scope("ga"):
+            gather_x(0, e, True).wait_recv()
+        send_halo(lax.rem(xi + e, nx))
+    for c in range(nx):
+        for p, y in ((0, 0), (1, rows - 1)):
+            r.joined[y + 1, pl.ds(c * cs, cs)] = r.gath[c, p]
     need_now("wmp")
-    for side, at, ok in ((0, 0, up_ok), (1, rows + 1, dn_ok)):
-        @pl.when(ok)
-        def _(side=side, at=at):
-            with scope("hw"):
-                arrived(r.halo.at[side], r.h_r.at[side])
-            for c in range(nx):
-                r.joined[at, pl.ds(c * cs, cs)] = r.halo[side, c]
     with scope("gb"):
         for g in range(1, n_cut):
             for e in range(1, nx):
@@ -584,14 +579,25 @@
                     r.gath[c, place_of[y]].astype(F32) * on[y].astype(F32)
                 ).astype(BF16)
 
+    def take_halo():
+        for side, at, ok in ((0, 0, up_ok), (1, rows + 1, dn_ok)):
+            @pl.when(ok)
+            def _(side=side, at=at):
+                with scope("hw"):
+                    arrived(r.halo.at[side], r.h_r.at[side])
+                for c in range(nx):
+                    r.joined[at, pl.ds(c * cs, cs)] = r.halo[side, c]
+
     def merged_copy(h):
         run = pl.ds(*halves[h])
         return rcopy(
             r.merged.at[run], r.merged_in.at[run], r.one_s.at[3], r.one_r.at[2], sect=peer
         )
 
-    halves = [(0, 2), (2, live - 2)]
+    halves = [(2, live - 2), (0, 2)]
     for h, (lo, n) in enumerate(halves):
+        if h == 1:
+            take_halo()
         with scope(f"merge{h}"):
             lhs = jnp.concatenate(
                 [

time: 27.9 us -> 26.7 us (0.957); the launches traced: 27.3 us -> 26.5 us
  Pallas kernels: 26.5 us -> 25.6 us
    pallas_call x1, Pallas kernels: 26.5 us -> 25.6 us  [shards(): pl.pallas_call(functools.partial(kernel, dims, names), out_shape=jax.Shap...]
where the time goes in v3:
time: 26.7 us; the launch traced here: 26.5 us
  Pallas kernels  25.6 us (96%)
  other arithmetic  0.85 us (3%)
    pallas_call x1, Pallas kernels, shards(): pl.pallas_call(functools.partial(kernel, dims, names), out_shape=jax.Shap...  25.6 us
    max x1, other arithmetic, shards(): return jnp.maximum(merged_map, jnp.zeros_like(merged_map))  0.85 us

profile of v3, /device:TPU:0, one launch (start us, length us, event | category | flops | bytes accessed | tf_op | source)
XLA Modules:
  0.0 26.5 jit_solution(579421468975228516)
XLA Ops:
  0.0 25.6 %shard_map.136 = bf16[2,6,96,256]{3,2,1,0:T(8,128)(2,1)S(1)} custom-call(s32[2,6]{1,0:T(2,128)} %refs_0_.1, bf16[2,6,96,512]{3,2,1,0:T(8,128)(2,1)} %refs_1_.1, bf16[2,6,96,256]{3,2,1,0:T(8,128)(2,1)} %refs_2_.1, bf16[512,256]{1,0:T(8,128)(2,1)} %refs_3_.1, bf16[3,3,3,512,256]{4,3,2,1,0:T(8,128)(2,1)} %refs_4_.1, f32[4,256]{1,0:T(4,128)} %refs_5_.1, ...), custom_call_target="tpu_custom_call" | custom-call | tf_op jit(solution)/shard_map/pallas_call | solution.py:749
  25.7 0.9 %broadcast_maximum_fusion = bf16[2,6,96,256]{3,2,1,0:T(8,128)(2,1)} fusion(bf16[2,6,96,256]{3,2,1,0:T(8,128)(2,1)S(1)} %shard_map.136), kind=kLoop, calls=%fused_computation | loop fusion | flops 294912 | bytes 1179648 | tf_op jit(solution)/shard_map/max | solution.py:759

commit v4 on v3

--- a/solution.py
+++ b/solution.py
@@ -388,13 +388,20 @@
         need_now("off")
     with scope("offa"):
         for_off(off_theirs)
+    need_now("taps0")
+    own_half(1, 0)
     with scope("offb"):
         for_off(first, 1)
     with scope("offs0"):
         for_off(off_send, 0)
-    need_now("taps0")
-    own_half(1, 0)
     own_half(1, 1)
+    with scope("second1"):
+        second(1)
+    send_x(1, 0)
+    with scope("offs1"):
+        for_off(off_send, 1)
+    for g in range(1, n_cut):
+        send_x(1, g)
     with scope("poolb"):
         arrived(all_of(r.pool_s, ns - 1), r.one_r.at[0])
         total = r.pool_s[0]
@@ -403,22 +410,13 @@
         r.pool_b[band] = total
     for e in range(1, nb):
         pool_band(e).start()
-    with scope("second1"):
-        second(1)
-    send_x(1, 0)
-    with scope("offs1"):
-        for_off(off_send, 1)
-    for g in range(1, n_cut):
-        send_x(1, g)
     need_now("taps1")
     own_half(2, 0)
+    own_half(3, 0)
     own_half(2, 1)
-    own_half(3, 0)
     with scope("second2"):
         second(2)
     send_x(2, 0)
-    with scope("fwd0"):
-        for_off(forward_off, 0)
     own_half(3, 1)
     with scope("second3"):
         second(3)
@@ -426,6 +424,8 @@
     for t in (2, 3):
         for g in range(1, n_cut):
             send_x(t, g)
+    with scope("fwd0"):
+        for_off(forward_off, 0)
 
     with scope("low"):
         need_now("low", "wr", "br", "wml", "vec")

time: 26.7 us -> 26.2 us (0.981)
  Pallas kernels: 25.6 us -> 25.2 us
    pallas_call x1, Pallas kernels: 25.6 us -> 25.2 us  [shards(): pl.pallas_call(functools.partial(kernel, dims, names), out_shape=jax.Shap...]
where the time goes in v4:
time: 26.2 us; the launch traced here: 26.1 us
  Pallas kernels  25.2 us (96%)
  other arithmetic  0.85 us (3%)
    pallas_call x1, Pallas kernels, shards(): pl.pallas_call(functools.partial(kernel, dims, names), out_shape=jax.Shap...  25.2 us
    max x1, other arithmetic, shards(): return jnp.maximum(merged_map, jnp.zeros_like(merged_map))  0.85 us

profile of v4, /device:TPU:0, one launch (start us, length us, event | category | flops | bytes accessed | tf_op | source)
XLA Modules:
  0.0 26.1 jit_solution(11130311984357168370)
XLA Ops:
  0.0 25.2 %shard_map.136 = bf16[2,6,96,256]{3,2,1,0:T(8,128)(2,1)S(1)} custom-call(s32[2,6]{1,0:T(2,128)} %refs_0_.1, bf16[2,6,96,512]{3,2,1,0:T(8,128)(2,1)} %refs_1_.1, bf16[2,6,96,256]{3,2,1,0:T(8,128)(2,1)} %refs_2_.1, bf16[512,256]{1,0:T(8,128)(2,1)} %refs_3_.1, bf16[3,3,3,512,256]{4,3,2,1,0:T(8,128)(2,1)} %refs_4_.1, f32[4,256]{1,0:T(4,128)} %refs_5_.1, ...), custom_call_target="tpu_custom_call" | custom-call | tf_op jit(solution)/shard_map/pallas_call | solution.py:749
  25.2 0.9 %broadcast_maximum_fusion = bf16[2,6,96,256]{3,2,1,0:T(8,128)(2,1)} fusion(bf16[2,6,96,256]{3,2,1,0:T(8,128)(2,1)S(1)} %shard_map.136), kind=kLoop, calls=%fused_computation | loop fusion | flops 294912 | bytes 1179648 | tf_op jit(solution)/shard_map/max | solution.py:759

commit v5 on v4

--- a/solution.py
+++ b/solution.py
@@ -112,8 +112,22 @@
 
     for e in range(1, ns):
         hello(band, lax.rem(sect + e, ns))
-    for e in range(1, nb):
-        hello(lax.rem(band + e, nb), sect)
+    for ok, step in ((up_ok, -1), (dn_ok, 1)):
+        @pl.when(ok)
+        def _(step=step):
+            hello(band + step, sect)
+
+    def pass_on(sem, step, ok):
+        @pl.when(jnp.logical_and(jnp.logical_and(up_ok, dn_ok), ok))
+        def _():
+            pl.semaphore_signal(
+                sem, inc=1, device_id={"band": band + step, "sect": sect}, device_id_type=MESH
+            )
+
+    def word_from(sem, ok):
+        @pl.when(ok)
+        def _():
+            pl.semaphore_wait(sem, 1)
 
     def rcopy(src, dst, s, rs, **where):
         return pltpu.make_async_remote_copy(
@@ -361,12 +375,18 @@
     with scope("first0a"):
         first(0, 0)
     with scope("bar"):
-        pl.semaphore_wait(bar, (ns - 1) + (nb - 1))
+        sides = jnp.minimum(band, 1) + jnp.minimum(nb - 1 - band, 1)
+        pl.semaphore_wait(bar, (ns - 1) + sides)
     core_copy(0).start()
-    for t in range(4, 4 + n_off):
-        @pl.when(gets_from(t))
-        def _(t=t):
-            sel_copy(t).start()
+    pass_on(r.above, 1, band < 2)
+    pass_on(r.below, -1, band + 2 >= nb)
+
+    def tell(i, ok):
+        for t in range(4, 4 + n_off):
+            if off[t - 4][1] == i:
+                @pl.when(jnp.logical_and(gets_from(t), ok))
+                def _(t=t):
+                    sel_copy(t).start()
 
     @pl.when(up_ok)
     def _():
@@ -384,12 +404,20 @@
         second(0)
     for g in range(n_cut):
         send_x(0, g)
+    with scope("p1"):
+        word_from(r.above, band >= 2)
+    pass_on(r.above, 1, band >= 2)
+    tell(0, band >= 0)
     if n_off:
         need_now("off")
     with scope("offa"):
         for_off(off_theirs)
     need_now("taps0")
     own_half(1, 0)
+    with scope("p2"):
+        word_from(r.below, jnp.logical_and(up_ok, band + 2 < nb))
+    pass_on(r.below, -1, band + 2 < nb)
+    tell(2, up_ok)
     with scope("offb"):
         for_off(first, 1)
     with scope("offs0"):
@@ -397,11 +425,11 @@
     own_half(1, 1)
     with scope("second1"):
         second(1)
-    send_x(1, 0)
-    with scope("offs1"):
-        for_off(off_send, 1)
-    for g in range(1, n_cut):
+    for g in range(n_cut):
         send_x(1, g)
+    with scope("p3"):
+        word_from(r.below, jnp.logical_and(jnp.logical_not(up_ok), band + 2 < nb))
+    tell(2, jnp.logical_not(up_ok))
     with scope("poolb"):
         arrived(all_of(r.pool_s, ns - 1), r.one_r.at[0])
         total = r.pool_s[0]
@@ -414,6 +442,8 @@
     own_half(2, 0)
     own_half(3, 0)
     own_half(2, 1)
+    with scope("offs1"):
+        for_off(off_send, 1)
     with scope("second2"):
         second(2)
     send_x(2, 0)
@@ -728,6 +758,8 @@
         lowacc=vm((live, cols, dec), F32),
         merged=vm((live, cols, dec), BF16),
         merged_in=vm((live, cols, dec), BF16),
+        above=pltpu.SemaphoreType.REGULAR,
+        below=pltpu.SemaphoreType.REGULAR,
         loc_sem=dma((16,)),
         one_s=dma((4,)),
         one_r=dma((3,)),

time: 26.2 us -> 25.2 us (0.962)
  Pallas kernels: 25.2 us -> 24.2 us
    pallas_call x1, Pallas kernels: 25.2 us -> 24.2 us  [shards(): pl.pallas_call(functools.partial(kernel, dims, names), out_shape=jax.Shap...]
where the time goes in v5:
time: 25.2 us; the launch traced here: 25.1 us
  Pallas kernels  24.2 us (96%)
  other arithmetic  0.85 us (3%)
    pallas_call x1, Pallas kernels, shards(): pl.pallas_call(functools.partial(kernel, dims, names), out_shape=jax.Shap...  24.2 us
    max x1, other arithmetic, shards(): return jnp.maximum(merged_map, jnp.zeros_like(merged_map))  0.85 us

profile of v5, /device:TPU:0, one launch (start us, length us, event | category | flops | bytes accessed | tf_op | source)
XLA Modules:
  0.0 25.1 jit_solution(12299400426110377195)
XLA Ops:
  0.0 24.2 %shard_map.136 = bf16[2,6,96,256]{3,2,1,0:T(8,128)(2,1)S(1)} custom-call(s32[2,6]{1,0:T(2,128)} %refs_0_.1, bf16[2,6,96,512]{3,2,1,0:T(8,128)(2,1)} %refs_1_.1, bf16[2,6,96,256]{3,2,1,0:T(8,128)(2,1)} %refs_2_.1, bf16[512,256]{1,0:T(8,128)(2,1)} %refs_3_.1, bf16[3,3,3,512,256]{4,3,2,1,0:T(8,128)(2,1)} %refs_4_.1, f32[4,256]{1,0:T(4,128)} %refs_5_.1, ...), custom_call_target="tpu_custom_call" | custom-call | tf_op jit(solution)/shard_map/pallas_call | solution.py:781
  24.2 0.9 %broadcast_maximum_fusion = bf16[2,6,96,256]{3,2,1,0:T(8,128)(2,1)} fusion(bf16[2,6,96,256]{3,2,1,0:T(8,128)(2,1)S(1)} %shard_map.136), kind=kLoop, calls=%fused_computation | loop fusion | flops 294912 | bytes 1179648 | tf_op jit(solution)/shard_map/max | solution.py:791

commit v6 on v5

--- a/solution.py
+++ b/solution.py
@@ -60,6 +60,20 @@
     mine, theirs = core, 1 - core
     peer = xi * 2 + 1 - core
 
+    bar = pltpu.get_barrier_semaphore()
+    up_ok = band >= 1
+    dn_ok = band + 1 < nb
+
+    def hello(b, s):
+        pl.semaphore_signal(bar, inc=1, device_id={"band": b, "sect": s}, device_id_type=MESH)
+
+    for e in range(1, ns):
+        hello(band, lax.rem(sect + e, ns))
+    for ok, step in ((up_ok, -1), (dn_ok, 1)):
+        @pl.when(ok)
+        def _(step=step):
+            hello(band + step, sect)
+
     waits = {}
 
     def fetch(name, *copies, whole):
@@ -80,6 +94,261 @@
     fetch("w1", (r.w1_h, r.w1), whole=r.w1)
     fetch("mine", (r.feat_h.at[mine], r.feat_own), whole=r.feat_own)
     fetch("wpool", (r.wpool_h, r.wpool), whole=r.wpool)
+    def pass_on(sem, step, ok):
+        @pl.when(jnp.logical_and(jnp.logical_and(up_ok, dn_ok), ok))
+        def _():
+            pl.semaphore_signal(
+                sem, inc=1, device_id={"band": band + step, "sect": sect}, device_id_type=MESH
+            )
+
+    def word_from(sem, ok):
+        @pl.when(ok)
+        def _():
+            pl.semaphore_wait(sem, 1)
+
+    def rcopy(src, dst, s, rs, **where):
+        return pltpu.make_async_remote_copy(
+            src_ref=src, dst_ref=dst, send_sem=s, recv_sem=rs, device_id=where, device_id_type=MESH
+        )
+
+    low_up = rcopy(
+        r.low_h.at[mine, 0], r.low_halo.at[1], r.lo_s.at[0], r.lo_r.at[1], band=band - 1, sect=sect
+    )
+    low_dn = rcopy(
+        r.low_h.at[mine, rows - 1], r.low_halo.at[0], r.lo_s.at[1], r.lo_r.at[0],
+        band=band + 1, sect=sect,
+    )
+
+    def slots(m):
+        on = [r.mask[m, y] for y in range(rows)]
+        place_of = [0] + [None] * (rows - 2) + [1]
+        row_of = [0, rows - 1] + [jnp.int32(0)] * (live - 2)
+        hits = {}
+        count = jnp.int32(0)
+        for y in range(1, rows - 1):
+            place_of[y] = jnp.where(on[y] > 0, jnp.minimum(count + 2, live - 1), 0)
+            for p in range(2, live):
+                hit = jnp.logical_and(on[y] > 0, count == p - 2)
+                row_of[p] = jnp.where(hit, y, row_of[p])
+                hits[p, y] = jnp.where(hit, 1, 0)
+            count = count + on[y]
+        return on, place_of, row_of, hits
+
+    for ref in (r.m_l, r.m_r):
+        zero = jnp.zeros((ref.shape[0], pad, br_w), F32)
+        ref[:, :pad] = zero
+        ref[:, pad + cols :] = zero
+    for at in (0, rows + 1):
+        r.joined[at] = jnp.zeros((cols, br_w), BF16)
+
+    def taps(lhs, n, wref, d):
+        mid = jnp.dot(lhs, wref[1], preferred_element_type=F32).reshape(n, cols, br_w)
+        r.m_l[:n, pl.ds(pad, cols)] = jnp.dot(
+            lhs, wref[0], preferred_element_type=F32
+        ).reshape(n, cols, br_w)
+        r.m_r[:n, pl.ds(pad, cols)] = jnp.dot(
+            lhs, wref[2], preferred_element_type=F32
+        ).reshape(n, cols, br_w)
+        return mid + r.m_l[:n, pl.ds(pad - d, cols)] + r.m_r[:n, pl.ds(pad + d, cols)]
+
+    def core_copy(t):
+        if t < 4:
+            src, dst = r.part_own.at[t, 0], r.crecv_own.at[t]
+        else:
+            src, dst = r.part_off.at[t - 4, 0], r.crecv_off.at[t - 4]
+        return rcopy(src, dst, r.c_s.at[max(t - 3, 0)], r.c_r.at[t], sect=peer)
+
+    def run_of(t, g):
+        return cuts[g] if t < 4 else off_cuts[g]
+
+    def x_copy(t, g, e, incoming=False):
+        lo, n = run_of(t, g)
+        at = g * 2 + t // 3 if t < 4 else 2 * n_cut + (t - 4) * 2 + g
+        send, recv, u = (
+            (r.xsend_own, r.xrecv_own, t) if t < 4 else (r.xsend_off, r.xrecv_off, t - 4)
+        )
+        other = lax.rem(xi + e, nx)
+        slot = other if incoming else xi
+        return rcopy(
+            send.at[u, other, pl.ds(lo, n)], recv.at[u, slot, pl.ds(lo, n)],
+            r.x_s.at[max(t - 3, 0)], r.x_r.at[at, (e if incoming else nx - e) - 1],
+            sect=other * 2 + core,
+        )
+
+    def x_arrived(g):
+        for e in range(1, nx):
+            whole = r.xrecv_own.at[pl.ds(0, 3), lax.rem(xi + e, nx), pl.ds(*cuts[g])]
+            arrived(whole, r.x_r.at[g * 2, e - 1])
+
+    def send_x(t, g):
+        for e in range(1, nx):
+            x_copy(t, g, e).start()
+
+    def first(t, step):
+        image = r.feat.at[0] if step == 0 else r.feat_own
+        if t < 4:
+            k = ORDER[t]
+            row_of = facts[step][2]
+            lhs = jnp.concatenate([image[row_of[p]] for p in range(live)], axis=0)
+            if k:
+                val = taps(lhs, live, r.wd.at[need.index((k, 1))], DILATIONS[k - 1])
+            else:
+                val = jnp.dot(lhs, r.w1[...], preferred_element_type=F32).reshape(live, cols, br_w)
+            r.part_own[t, step] = val.astype(BF16)
+        else:
+            k, i, _ = off[t - 4]
+            lhs = image[...].reshape(rows * cols, ch)
+            val = taps(lhs, rows, r.wd.at[need.index((k, i))], DILATIONS[k - 1])
+            r.part_off[t - 4, step] = val.astype(BF16)
+
+    def second(t):
+        core_copy(t).wait_recv()
+        for c in range(nx):
+            cell = pl.ds(c * cs, cs)
+            total = r.part_own[t, 1, :, cell].astype(F32) + r.crecv_own[t, :, cell].astype(F32)
+            r.xsend_own[t, c] = total.astype(BF16)
+
+            @pl.when(xi == c)
+            def _(total=total):
+                r.keep_own[t] = total
+
+    def second_off(t, h):
+        u = t - 4
+        if h == 0:
+            core_copy(t).wait_recv()
+        else:
+            sel_copy(t).wait_recv()
+        lo, n = off_cuts[h]
+        for c in range(nx):
+            cell = pl.ds(c * cs, cs)
+
+            def row(y, cell=cell):
+                return r.part_off[u, 1, y, cell].astype(F32) + r.crecv_off[u, y, cell].astype(F32)
+
+            if h == 0:
+                picked = [row(0), row(rows - 1)]
+            else:
+                inner = [row(y) for y in range(1, rows - 1)]
+                picked = []
+                for p in range(2, live):
+                    total = jnp.zeros((cs, br_w), F32)
+                    for y in range(1, rows - 1):
+                        at = (p - 2) * (rows - 2) + y - 1
+                        total = total + inner[y - 1] * r.sel_in[u, at : at + 1]
+                    picked.append(total)
+            for p, total in enumerate(picked):
+                r.xsend_off[u, c, lo + p] = total.astype(BF16)
+
+            @pl.when(xi == c)
+            def _(picked=picked):
+                for p, total in enumerate(picked):
+                    r.keep_off[u, lo + p] = total
+
+    def sends_to(t):
+        k, i, hop = off[t - 4]
+        return band + hop < nb if i == 0 else band - hop >= 0
+
+    def gets_from(t):
+        k, i, hop = off[t - 4]
+        return band - hop >= 0 if i == 0 else band + hop < nb
+
+    def sel_copy(t):
+        k, i, hop = off[t - 4]
+        return rcopy(
+            r.sel_out, r.sel_in.at[t - 4], r.s_s.at[t - 4], r.s_r.at[t - 4],
+            band=band - hop if i == 0 else band + hop, sect=sect,
+        )
+
+    def z_copy(t, h):
+        k, i, hop = off[t - 4]
+        run = pl.ds(*off_cuts[h])
+        return rcopy(
+            r.zsend.at[t - 4, run], r.zrecv.at[t - 4, run], r.z_s.at[t - 4], r.z_r.at[t - 4, h],
+            band=band + hop if i == 0 else band - hop, sect=sect,
+        )
+
+    def forward_off(t, h):
+        run = pl.ds(*off_cuts[h])
+        total = r.keep_off[t - 4, run]
+        for e in range(1, nx):
+            x_copy(t, h, e, True).wait_recv()
+            total = total + r.xrecv_off[t - 4, lax.rem(xi + e, nx), run].astype(F32)
+        r.zsend[t - 4, run] = total.astype(BF16)
+        z_copy(t, h).start()
+
+    def for_off(fn, *rest):
+        for t in range(4, 4 + n_off):
+            @pl.when(sends_to(t))
+            def _(t=t):
+                fn(t, *rest)
+
+    def pool_sect(e, incoming=False):
+        other = lax.rem(sect + e, ns)
+        slot = other if incoming else sect
+        return rcopy(
+            r.pool_s.at[sect], r.pool_s.at[slot], r.one_s.at[0], r.one_r.at[0], sect=other
+        )
+
+    def pool_band(e, incoming=False):
+        other = lax.rem(band + e, nb)
+        slot = other if incoming else band
+        return rcopy(
+            r.pool_b.at[band], r.pool_b.at[slot], r.one_s.at[1], r.one_r.at[1], band=other
+        )
+
+    def dot_f32(v, w):
+        n = v.shape[0]
+        high = v.astype(BF16).astype(F32)
+        middle = (v - high).astype(BF16).astype(F32)
+        terms = jnp.concatenate([high, middle, v - high - middle], axis=0).astype(BF16)
+        p = jnp.dot(terms, w, preferred_element_type=F32)
+        return p[:n] + p[n : 2 * n] + p[2 * n :]
+
+    def all_of(ref, n):
+        return ref.at[pl.ds(0, n)]
+
+    def arrived(whole, sem):
+        pltpu.make_async_copy(whole, whole, sem).wait()
+
+    def pool():
+        need_now("wpool")
+        ones = jnp.ones((8, rows * cols), BF16)
+        at = lax.broadcasted_iota(jnp.int32, (8, ch), 0)
+        sums = jnp.zeros((8, ch), F32)
+        for m, image in ((mine, r.feat_own), (theirs, r.feat.at[0])):
+            part = jnp.dot(
+                ones, image[...].reshape(rows * cols, ch), preferred_element_type=F32
+            )
+            sums = jnp.where(at == m, part, sums)
+        r.pool_s[sect] = dot_f32(sums, r.wpool[...])[:mb]
+        for e in range(1, ns):
+            pool_sect(e).start()
+
+    need_now("mask")
+    facts = [slots(theirs), slots(mine)]
+    on, place_of, row_of, hits = facts[1]
+
+    for p in range(2, live):
+        for y in range(1, rows - 1):
+            at = (p - 2) * (rows - 2) + y - 1
+            r.sel_out[at : at + 1] = jnp.full((1, br_w), hits[p, y].astype(F32))
+
+    def own_half(t, step):
+        with scope(f"first{t}{'ab'[step]}"):
+            first(t, step)
+        if step == 0:
+            core_copy(t).start()
+
+    def off_theirs(t):
+        first(t, 0)
+        core_copy(t).start()
+
+    def off_send(t, h):
+        second_off(t, h)
+        send_x(t, h)
+
+    with scope("w0"):
+        need_now("theirs", "w1")
     if n_off:
         fetch("off", *[taps_of(*n) for n in need[3:]], whole=r.wd.at[pl.ds(3, n_off)])
     fetch("taps0", taps_of(*need[0]), whole=r.wd.at[0])
@@ -102,282 +371,16 @@
         ],
         whole=r.wmp,
     )
-
-    bar = pltpu.get_barrier_semaphore()
-    up_ok = band >= 1
-    dn_ok = band + 1 < nb
-
-    def hello(b, s):
-        pl.semaphore_signal(bar, inc=1, device_id={"band": b, "sect": s}, device_id_type=MESH)
-
-    for e in range(1, ns):
-        hello(band, lax.rem(sect + e, ns))
-    for ok, step in ((up_ok, -1), (dn_ok, 1)):
-        @pl.when(ok)
-        def _(step=step):
-            hello(band + step, sect)
-
-    def pass_on(sem, step, ok):
-        @pl.when(jnp.logical_and(jnp.logical_and(up_ok, dn_ok), ok))
-        def _():
-            pl.semaphore_signal(
-                sem, inc=1, device_id={"band": band + step, "sect": sect}, device_id_type=MESH
-            )
-
-    def word_from(sem, ok):
-        @pl.when(ok)
-        def _():
-            pl.semaphore_wait(sem, 1)
-
-    def rcopy(src, dst, s, rs, **where):
-        return pltpu.make_async_remote_copy(
-            src_ref=src, dst_ref=dst, send_sem=s, recv_sem=rs, device_id=where, device_id_type=MESH
-        )
-
-    low_up = rcopy(
-        r.low_h.at[mine, 0], r.low_halo.at[1], r.lo_s.at[0], r.lo_r.at[1], band=band - 1, sect=sect
-    )
-    low_dn = rcopy(
-        r.low_h.at[mine, rows - 1], r.low_halo.at[0], r.lo_s.at[1], r.lo_r.at[0],
-        band=band + 1, sect=sect,
-    )
-
-    def slots(m):
-        on = [r.mask[m, y] for y in range(rows)]
-        place_of = [0] + [None] * (rows - 2) + [1]
-        row_of = [0, rows - 1] + [jnp.int32(0)] * (live - 2)
-        hits = {}
-        count = jnp.int32(0)
-        for y in range(1, rows - 1):
-            place_of[y] = jnp.where(on[y] > 0, jnp.minimum(count + 2, live - 1), 0)
-            for p in range(2, live):
-                hit = jnp.logical_and(on[y] > 0, count == p - 2)
-                row_of[p] = jnp.where(hit, y, row_of[p])
-                hits[p, y] = jnp.where(hit, 1, 0)
-            count = count + on[y]
-        return on, place_of, row_of, hits
-
-    for ref in (r.m_l, r.m_r):
-        zero = jnp.zeros((ref.shape[0], pad, br_w), F32)
-        ref[:, :pad] = zero
-        ref[:, pad + cols :] = zero
-    for at in (0, rows + 1):
-        r.joined[at] = jnp.zeros((cols, br_w), BF16)
-
-    def taps(lhs, n, wref, d):
-        mid = jnp.dot(lhs, wref[1], preferred_element_type=F32).reshape(n, cols, br_w)
-        r.m_l[:n, pl.ds(pad, cols)] = jnp.dot(
-            lhs, wref[0], preferred_element_type=F32
-        ).reshape(n, cols, br_w)
-        r.m_r[:n, pl.ds(pad, cols)] = jnp.dot(
-            lhs, wref[2], preferred_element_type=F32
-        ).reshape(n, cols, br_w)
-        return mid + r.m_l[:n, pl.ds(pad - d, cols)] + r.m_r[:n, pl.ds(pad + d, cols)]
-
-    def core_copy(t):
-        if t < 4:
-            src, dst = r.part_own.at[t, 0], r.crecv_own.at[t]
-        else:
-            src, dst = r.part_off.at[t - 4, 0], r.crecv_off.at[t - 4]
-        return rcopy(src, dst, r.c_s.at[max(t - 3, 0)], r.c_r.at[t], sect=peer)
-
-    def run_of(t, g):
-        return cuts[g] if t < 4 else off_cuts[g]
-
-    def x_copy(t, g, e, incoming=False):
-        lo, n = run_of(t, g)
-        at = g * 2 + t // 3 if t < 4 else 2 * n_cut + (t - 4) * 2 + g
-        send, recv, u = (
-            (r.xsend_own, r.xrecv_own, t) if t < 4 else (r.xsend_off, r.xrecv_off, t - 4)
-        )
-        other = lax.rem(xi + e, nx)
-        slot = other if incoming else xi
-        return rcopy(
-            send.at[u, other, pl.ds(lo, n)], recv.at[u, slot, pl.ds(lo, n)],
-            r.x_s.at[max(t - 3, 0)], r.x_r.at[at, (e if incoming else nx - e) - 1],
-            sect=other * 2 + core,
-        )
-
-    def x_arrived(g):
-        for e in range(1, nx):
-            whole = r.xrecv_own.at[pl.ds(0, 3), lax.rem(xi + e, nx), pl.ds(*cuts[g])]
-            arrived(whole, r.x_r.at[g * 2, e - 1])
-
-    def send_x(t, g):
-        for e in range(1, nx):
-            x_copy(t, g, e).start()
-
-    def first(t, step):
-        image = r.feat.at[0] if step == 0 else r.feat_own
-        if t < 4:
-            k = ORDER[t]
-            row_of = facts[step][2]
-            lhs = jnp.concatenate([image[row_of[p]] for p in range(live)], axis=0)
-            if k:
-                val = taps(lhs, live, r.wd.at[need.index((k, 1))], DILATIONS[k - 1])
-            else:
-                val = jnp.dot(lhs, r.w1[...], preferred_element_type=F32).reshape(live, cols, br_w)
-            r.part_own[t, step] = val.astype(BF16)
-        else:
-            k, i, _ = off[t - 4]
-            lhs = image[...].reshape(rows * cols, ch)
-            val = taps(lhs, rows, r.wd.at[need.index((k, i))], DILATIONS[k - 1])
-            r.part_off[t - 4, step] = val.astype(BF16)
-
-    def second(t):
-        core_copy(t).wait_recv()
-        for c in range(nx):
-            cell = pl.ds(c * cs, cs)
-            total = r.part_own[t, 1, :, cell].astype(F32) + r.crecv_own[t, :, cell].astype(F32)
-            r.xsend_own[t, c] = total.astype(BF16)
-
-            @pl.when(xi == c)
-            def _(total=total):
-                r.keep_own[t] = total
-
-    def second_off(t, h):
-        u = t - 4
-        if h == 0:
-            core_copy(t).wait_recv()
-        else:
-            sel_copy(t).wait_recv()
-        lo, n = off_cuts[h]
-        for c in range(nx):
-            cell = pl.ds(c * cs, cs)
-
-            def row(y, cell=cell):
-                return r.part_off[u, 1, y, cell].astype(F32) + r.crecv_off[u, y, cell].astype(F32)
-
-            if h == 0:
-                picked = [row(0), row(rows - 1)]
-            else:
-                inner = [row(y) for y in range(1, rows - 1)]
-                picked = []
-                for p in range(2, live):
-                    total = jnp.zeros((cs, br_w), F32)
-                    for y in range(1, rows - 1):
-                        at = (p - 2) * (rows - 2) + y - 1
-                        total = total + inner[y - 1] * r.sel_in[u, at : at + 1]
-                    picked.append(total)
-            for p, total in enumerate(picked):
-                r.xsend_off[u, c, lo + p] = total.astype(BF16)
-
-            @pl.when(xi == c)
-            def _(picked=picked):
-                for p, total in enumerate(picked):
-                    r.keep_off[u, lo + p] = total
-
-    def sends_to(t):
-        k, i, hop = off[t - 4]
-        return band + hop < nb if i == 0 else band - hop >= 0
-
-    def gets_from(t):
-        k, i, hop = off[t - 4]
-        return band - hop >= 0 if i == 0 else band + hop < nb
-
-    def sel_copy(t):
-        k, i, hop = off[t - 4]
-        return rcopy(
-            r.sel_out, r.sel_in.at[t - 4], r.s_s.at[t - 4], r.s_r.at[t - 4],
-            band=band - hop if i == 0 else band + hop, sect=sect,
-        )
-
-    def z_copy(t, h):
-        k, i, hop = off[t - 4]
-        run = pl.ds(*off_cuts[h])
-        return rcopy(
-            r.zsend.at[t - 4, run], r.zrecv.at[t - 4, run], r.z_s.at[t - 4], r.z_r.at[t - 4, h],
-            band=band + hop if i == 0 else band - hop, sect=sect,
-        )
-
-    def forward_off(t, h):
-        run = pl.ds(*off_cuts[h])
-        total = r.keep_off[t - 4, run]
-        for e in range(1, nx):
-            x_copy(t, h, e, True).wait_recv()
-            total = total + r.xrecv_off[t - 4, lax.rem(xi + e, nx), run].astype(F32)
-        r.zsend[t - 4, run] = total.astype(BF16)
-        z_copy(t, h).start()
-
-    def for_off(fn, *rest):
-        for t in range(4, 4 + n_off):
-            @pl.when(sends_to(t))
-            def _(t=t):
-                fn(t, *rest)
-
-    def pool_sect(e, incoming=False):
-        other = lax.rem(sect + e, ns)
-        slot = other if incoming else sect
-        return rcopy(
-            r.pool_s.at[sect], r.pool_s.at[slot], r.one_s.at[0], r.one_r.at[0], sect=other
-        )
-
-    def pool_band(e, incoming=False):
-        other = lax.rem(band + e, nb)
-        slot = other if incoming else band
-        return rcopy(
-            r.pool_b.at[band], r.pool_b.at[slot], r.one_s.at[1], r.one_r.at[1], band=other
-        )
-
-    def dot_f32(v, w):
-        n = v.shape[0]
-        high = v.astype(BF16).astype(F32)
-        middle = (v - high).astype(BF16).astype(F32)
-        terms = jnp.concatenate([high, middle, v - high - middle], axis=0).astype(BF16)
-        p = jnp.dot(terms, w, preferred_element_type=F32)
-        return p[:n] + p[n : 2 * n] + p[2 * n :]
-
-    def all_of(ref, n):
-        return ref.at[pl.ds(0, n)]
-
-    def arrived(whole, sem):
-        pltpu.make_async_copy(whole, whole, sem).wait()
-
-    def pool():
-        need_now("wpool")
-        ones = jnp.ones((8, rows * cols), BF16)
-        at = lax.broadcasted_iota(jnp.int32, (8, ch), 0)
-        sums = jnp.zeros((8, ch), F32)
-        for m, image in ((mine, r.feat_own), (theirs, r.feat.at[0])):
-            part = jnp.dot(
-                ones, image[...].reshape(rows * cols, ch), preferred_element_type=F32
-            )
-            sums = jnp.where(at == m, part, sums)
-        r.pool_s[sect] = dot_f32(sums, r.wpool[...])[:mb]
-        for e in range(1, ns):
-            pool_sect(e).start()
-
-    need_now("mask")
-    facts = [slots(theirs), slots(mine)]
-    on, place_of, row_of, hits = facts[1]
-
-    for p in range(2, live):
-        for y in range(1, rows - 1):
-            at = (p - 2) * (rows - 2) + y - 1
-            r.sel_out[at : at + 1] = jnp.full((1, br_w), hits[p, y].astype(F32))
-
-    def own_half(t, step):
-        with scope(f"first{t}{'ab'[step]}"):
-            first(t, step)
-        if step == 0:
-            core_copy(t).start()
-
-    def off_theirs(t):
-        first(t, 0)
-        core_copy(t).start()
-
-    def off_send(t, h):
-        second_off(t, h)
-        send_x(t, h)
-
-    with scope("w0"):
-        need_now("theirs", "w1")
     with scope("first0a"):
         first(0, 0)
     with scope("bar"):
         sides = jnp.minimum(band, 1) + jnp.minimum(nb - 1 - band, 1)
         pl.semaphore_wait(bar, (ns - 1) + sides)
     core_copy(0).start()
+    for e in range(1, nx):
+        pl.semaphore_signal(
+            r.across, inc=1, device_id={"sect": lax.rem(sect + 2 * e, ns)}, device_id_type=MESH
+        )
     pass_on(r.above, 1, band < 2)
     pass_on(r.below, -1, band + 2 >= nb)
 
@@ -412,24 +415,24 @@
         need_now("off")
     with scope("offa"):
         for_off(off_theirs)
-    need_now("taps0")
-    own_half(1, 0)
     with scope("p2"):
         word_from(r.below, jnp.logical_and(up_ok, band + 2 < nb))
     pass_on(r.below, -1, band + 2 < nb)
     tell(2, up_ok)
+    need_now("taps0")
+    own_half(1, 0)
     with scope("offb"):
         for_off(first, 1)
     with scope("offs0"):
         for_off(off_send, 0)
+    with scope("p3"):
+        word_from(r.below, jnp.logical_and(jnp.logical_not(up_ok), band + 2 < nb))
+    tell(2, jnp.logical_not(up_ok))
     own_half(1, 1)
     with scope("second1"):
         second(1)
-    for g in range(n_cut):
+    for g in range(n_cut - 1):
         send_x(1, g)
-    with scope("p3"):
-        word_from(r.below, jnp.logical_and(jnp.logical_not(up_ok), band + 2 < nb))
-    tell(2, jnp.logical_not(up_ok))
     with scope("poolb"):
         arrived(all_of(r.pool_s, ns - 1), r.one_r.at[0])
         total = r.pool_s[0]
@@ -444,6 +447,7 @@
     own_half(2, 1)
     with scope("offs1"):
         for_off(off_send, 1)
+    send_x(1, n_cut - 1)
     with scope("second2"):
         second(2)
     send_x(2, 0)
@@ -568,32 +572,33 @@
             if lo + p < 2:
                 v = v * on[(0, rows - 1)[lo + p]].astype(F32)
             r.gath[xi, lo + p] = v.astype(BF16)
+        if g == 0:
+            if nx > 1:
+                pl.semaphore_wait(r.across, nx - 1)
+            for e in reversed(range(nx)):
+                for side, ok in ((0, dn_ok), (1, up_ok)):
+                    @pl.when(ok)
+                    def _(side=side, e=e):
+                        halo_copy(side, e).start()
         for e in range(1, nx):
             gather_x(g, e).start()
 
-    def halo_copy(side, c):
+    def halo_copy(side, e):
+        other = lax.rem(xi + e, nx)
         return rcopy(
-            r.gath.at[c, 1 - side], r.halo.at[side, c], r.h_s.at[side], r.h_r.at[side],
-            band=band + 1 if side == 0 else band - 1, sect=sect,
-        )
-
-    def send_halo(c):
-        for side, ok in ((0, dn_ok), (1, up_ok)):
-            @pl.when(ok)
-            def _(side=side):
-                halo_copy(side, c).start()
+            r.gath.at[xi, 1 - side], r.halo.at[side, xi], r.h_s.at[side], r.h_r.at[side],
+            band=band + 1 if side == 0 else band - 1, sect=other * 2 + core,
+        )
 
     early(0)
     project(0)
-    send_halo(xi)
     for g in range(1, n_cut):
         early(g)
     for g in range(1, n_cut):
         project(g)
-    for e in range(1, nx):
-        with scope("ga"):
+    with scope("ga"):
+        for e in range(1, nx):
             gather_x(0, e, True).wait_recv()
-        send_halo(lax.rem(xi + e, nx))
     for c in range(nx):
         for p, y in ((0, 0), (1, rows - 1)):
             r.joined[y + 1, pl.ds(c * cs, cs)] = r.gath[c, p]
@@ -758,6 +763,7 @@
         lowacc=vm((live, cols, dec), F32),
         merged=vm((live, cols, dec), BF16),
         merged_in=vm((live, cols, dec), BF16),
+        across=pltpu.SemaphoreType.REGULAR,
         above=pltpu.SemaphoreType.REGULAR,
         below=pltpu.SemaphoreType.REGULAR,
         loc_sem=dma((16,)),

time: 25.2 us -> 24.6 us (0.976)
  Pallas kernels: 24.2 us -> 23.6 us
    pallas_call x1, Pallas kernels: 24.2 us -> 23.6 us  [shards(): pl.pallas_call(functools.partial(kernel, dims, names), out_shape=jax.Shap...]
where the time goes in v6:
time: 24.6 us; the launch traced here: 24.4 us
  Pallas kernels  23.6 us (96%)
  other arithmetic  0.85 us (3%)
    pallas_call x1, Pallas kernels, shards(): pl.pallas_call(functools.partial(kernel, dims, names), out_shape=jax.Shap...  23.6 us
    max x1, other arithmetic, shards(): return jnp.maximum(merged_map, jnp.zeros_like(merged_map))  0.85 us

profile of v6, /device:TPU:0, one launch (start us, length us, event | category | flops | bytes accessed | tf_op | source)
XLA Modules:
  0.0 24.4 jit_solution(4168137768928485603)
XLA Ops:
  0.0 23.6 %shard_map.136 = bf16[2,6,96,256]{3,2,1,0:T(8,128)(2,1)S(1)} custom-call(s32[2,6]{1,0:T(2,128)} %refs_0_.1, bf16[2,6,96,512]{3,2,1,0:T(8,128)(2,1)} %refs_1_.1, bf16[2,6,96,256]{3,2,1,0:T(8,128)(2,1)} %refs_2_.1, bf16[512,256]{1,0:T(8,128)(2,1)} %refs_3_.1, bf16[3,3,3,512,256]{4,3,2,1,0:T(8,128)(2,1)} %refs_4_.1, f32[4,256]{1,0:T(4,128)} %refs_5_.1, ...), custom_call_target="tpu_custom_call" | custom-call | tf_op jit(solution)/shard_map/pallas_call | solution.py:787
  23.6 0.9 %broadcast_maximum_fusion = bf16[2,6,96,256]{3,2,1,0:T(8,128)(2,1)} fusion(bf16[2,6,96,256]{3,2,1,0:T(8,128)(2,1)S(1)} %shard_map.136), kind=kLoop, calls=%fused_computation | loop fusion | flops 294912 | bytes 1179648 | tf_op jit(solution)/shard_map/max | solution.py:797

commit v7 on v6

--- a/solution.py
+++ b/solution.py
@@ -48,7 +48,6 @@
     n_off = len(off)
     cuts = pieces(live)
     n_cut = len(cuts)
-    off_cuts = [(0, 2), (2, live - 2)]
     need = [(k, 1) for k in ORDER if k] + [(k, i) for k, i, _ in off]
     pad = (r.m_l.shape[1] - cols) // 2
     scope = jax.named_scope
@@ -93,7 +92,8 @@
     fetch("theirs", (r.feat_h.at[theirs], r.feat.at[0]), whole=r.feat.at[0])
     fetch("w1", (r.w1_h, r.w1), whole=r.w1)
     fetch("mine", (r.feat_h.at[mine], r.feat_own), whole=r.feat_own)
-    fetch("wpool", (r.wpool_h, r.wpool), whole=r.wpool)
+    if n_off:
+        fetch("off", *[taps_of(*n) for n in need[3:]], whole=r.wd.at[pl.ds(3, n_off)])
     def pass_on(sem, step, ok):
         @pl.when(jnp.logical_and(jnp.logical_and(up_ok, dn_ok), ok))
         def _():
@@ -159,11 +159,11 @@
         return rcopy(src, dst, r.c_s.at[max(t - 3, 0)], r.c_r.at[t], sect=peer)
 
     def run_of(t, g):
-        return cuts[g] if t < 4 else off_cuts[g]
+        return cuts[g]
 
     def x_copy(t, g, e, incoming=False):
         lo, n = run_of(t, g)
-        at = g * 2 + t // 3 if t < 4 else 2 * n_cut + (t - 4) * 2 + g
+        at = g * 2 + t // 3 if t < 4 else (t - 2) * n_cut + g
         send, recv, u = (
             (r.xsend_own, r.xrecv_own, t) if t < 4 else (r.xsend_off, r.xrecv_off, t - 4)
         )
@@ -216,9 +216,9 @@
         u = t - 4
         if h == 0:
             core_copy(t).wait_recv()
-        else:
+        elif h == 1:
             sel_copy(t).wait_recv()
-        lo, n = off_cuts[h]
+        lo, n = cuts[h]
         for c in range(nx):
             cell = pl.ds(c * cs, cs)
 
@@ -230,7 +230,7 @@
             else:
                 inner = [row(y) for y in range(1, rows - 1)]
                 picked = []
-                for p in range(2, live):
+                for p in range(lo, lo + n):
                     total = jnp.zeros((cs, br_w), F32)
                     for y in range(1, rows - 1):
                         at = (p - 2) * (rows - 2) + y - 1
@@ -261,14 +261,14 @@
 
     def z_copy(t, h):
         k, i, hop = off[t - 4]
-        run = pl.ds(*off_cuts[h])
+        run = pl.ds(*cuts[h])
         return rcopy(
             r.zsend.at[t - 4, run], r.zrecv.at[t - 4, run], r.z_s.at[t - 4], r.z_r.at[t - 4, h],
             band=band + hop if i == 0 else band - hop, sect=sect,
         )
 
     def forward_off(t, h):
-        run = pl.ds(*off_cuts[h])
+        run = pl.ds(*cuts[h])
         total = r.keep_off[t - 4, run]
         for e in range(1, nx):
             x_copy(t, h, e, True).wait_recv()
@@ -349,8 +349,7 @@
 
     with scope("w0"):
         need_now("theirs", "w1")
-    if n_off:
-        fetch("off", *[taps_of(*n) for n in need[3:]], whole=r.wd.at[pl.ds(3, n_off)])
+    fetch("wpool", (r.wpool_h, r.wpool), whole=r.wpool)
     fetch("taps0", taps_of(*need[0]), whole=r.wd.at[0])
     fetch("taps1", *[taps_of(*n) for n in need[1:3]], whole=r.wd.at[pl.ds(1, 2)])
     fetch("low", (r.low_h.at[mine], r.low), whole=r.low)
@@ -401,38 +400,42 @@
 
     need_now("mine")
     own_half(0, 1)
-    with scope("pool"):
-        pool()
+    if n_off:
+        need_now("off")
+    with scope("offa"):
+        for_off(off_theirs)
     with scope("second0"):
         second(0)
-    for g in range(n_cut):
-        send_x(0, g)
+    send_x(0, 0)
     with scope("p1"):
         word_from(r.above, band >= 2)
     pass_on(r.above, 1, band >= 2)
     tell(0, band >= 0)
-    if n_off:
-        need_now("off")
-    with scope("offa"):
-        for_off(off_theirs)
+    with scope("pool"):
+        pool()
     with scope("p2"):
         word_from(r.below, jnp.logical_and(up_ok, band + 2 < nb))
     pass_on(r.below, -1, band + 2 < nb)
     tell(2, up_ok)
-    need_now("taps0")
-    own_half(1, 0)
     with scope("offb"):
         for_off(first, 1)
     with scope("offs0"):
         for_off(off_send, 0)
+    for g in range(1, n_cut):
+        send_x(0, g)
+    need_now("taps0", "taps1")
+    own_half(1, 0)
+    own_half(2, 0)
     with scope("p3"):
         word_from(r.below, jnp.logical_and(jnp.logical_not(up_ok), band + 2 < nb))
     tell(2, jnp.logical_not(up_ok))
     own_half(1, 1)
     with scope("second1"):
         second(1)
-    for g in range(n_cut - 1):
+    for g in range(n_cut):
         send_x(1, g)
+    own_half(3, 0)
+    own_half(2, 1)
     with scope("poolb"):
         arrived(all_of(r.pool_s, ns - 1), r.one_r.at[0])
         total = r.pool_s[0]
@@ -441,17 +444,13 @@
         r.pool_b[band] = total
     for e in range(1, nb):
         pool_band(e).start()
-    need_now("taps1")
-    own_half(2, 0)
-    own_half(3, 0)
-    own_half(2, 1)
-    with scope("offs1"):
-        for_off(off_send, 1)
-    send_x(1, n_cut - 1)
     with scope("second2"):
         second(2)
+    own_half(3, 1)
+    with scope("offs1"):
+        for g in range(1, n_cut):
+            for_off(off_send, g)
     send_x(2, 0)
-    own_half(3, 1)
     with scope("second3"):
         second(3)
     send_x(3, 0)
@@ -503,8 +502,9 @@
                 terms[j] = term if i == 0 else terms[j] + term
         r.lowacc[...] = combine(terms[1], terms[0], terms[2], live) + r.vec[0].reshape(1, 1, br_w)
 
-    with scope("fwd1"):
-        for_off(forward_off, 1)
+    for g in range(1, n_cut):
+        with scope(f"fwd{g}"):
+            for_off(forward_off, g)
 
     need_now("wproj", "bbr")
     with scope("ctx"):
@@ -534,8 +534,7 @@
                 @pl.when(gets_from(u))
                 def _(u=u):
                     with scope(f"z{g}"):
-                        if g < 2:
-                            z_copy(u, g).wait_recv()
+                        z_copy(u, g).wait_recv()
                     run = pl.ds(lo, n)
                     r.keep_own[t, run] = r.keep_own[t, run] + r.zrecv[u - 4, run].astype(F32)
         total = r.keep_own[t, lo : lo + n]
@@ -603,6 +602,26 @@
         for p, y in ((0, 0), (1, rows - 1)):
             r.joined[y + 1, pl.ds(c * cs, cs)] = r.gath[c, p]
     need_now("wmp")
+    def merge_terms(rows_in, first_tap, taps_in):
+        lhs = jnp.concatenate(
+            [jnp.concatenate([r.joined[y] for y in ys], axis=0) for ys in rows_in], axis=1
+        )
+        tap = pl.ds(first_tap * br_w, taps_in * br_w)
+        return [jnp.dot(lhs, r.wmp[j, tap], preferred_element_type=F32) for j in range(3)]
+
+    for side, at, ok in ((0, 0, up_ok), (1, rows + 1, dn_ok)):
+        @pl.when(ok)
+        def _(side=side, at=at):
+            with scope("hw"):
+                arrived(r.halo.at[side], r.h_r.at[side])
+            for c in range(nx):
+                r.joined[at, pl.ds(c * cs, cs)] = r.halo[side, c]
+
+    with scope("edge"):
+        upper = merge_terms([[0], [1]], 0, 2)
+        lower = merge_terms([[rows], [rows + 1]], 1, 2)
+        left, mid, right = [jnp.concatenate(p, axis=0) for p in zip(upper, lower)]
+        r.lowacc[:2] = r.lowacc[:2] + combine(mid, left, right, 2)
     with scope("gb"):
         for g in range(1, n_cut):
             for e in range(1, nx):
@@ -614,36 +633,25 @@
                     r.gath[c, place_of[y]].astype(F32) * on[y].astype(F32)
                 ).astype(BF16)
 
-    def take_halo():
-        for side, at, ok in ((0, 0, up_ok), (1, rows + 1, dn_ok)):
-            @pl.when(ok)
-            def _(side=side, at=at):
-                with scope("hw"):
-                    arrived(r.halo.at[side], r.h_r.at[side])
-                for c in range(nx):
-                    r.joined[at, pl.ds(c * cs, cs)] = r.halo[side, c]
-
     def merged_copy(h):
         run = pl.ds(*halves[h])
         return rcopy(
             r.merged.at[run], r.merged_in.at[run], r.one_s.at[3], r.one_r.at[2], sect=peer
         )
 
-    halves = [(2, live - 2), (0, 2)]
+    halves = [(2, live - 2), (0, 2)] if live > 2 else [(0, 2)]
     for h, (lo, n) in enumerate(halves):
-        if h == 1:
-            take_halo()
         with scope(f"merge{h}"):
-            lhs = jnp.concatenate(
-                [
-                    jnp.concatenate([r.joined[row_of[p] + i] for p in range(lo, lo + n)], axis=0)
-                    for i in range(3)
-                ],
-                axis=1,
-            )
-            left, mid, right = [
-                jnp.dot(lhs, r.wmp[j], preferred_element_type=F32) for j in range(3)
-            ]
+            if lo:
+                terms = merge_terms(
+                    [[row_of[p] + i for p in range(lo, lo + n)] for i in range(3)], 0, 3
+                )
+            else:
+                terms = [
+                    jnp.concatenate(p, axis=0)
+                    for p in zip(merge_terms([[2]], 2, 1), merge_terms([[rows - 1]], 0, 1))
+                ]
+            left, mid, right = terms
             total = combine(mid, left, right, n) + r.lowacc[lo : lo + n]
             r.merged[lo : lo + n] = jax.nn.relu(total).astype(BF16)
         merged_copy(h).start()
@@ -774,11 +782,11 @@
         c_s=dma((1 + n_off,)),
         c_r=dma((4 + n_off,)),
         x_s=dma((1 + n_off,)),
-        x_r=dma((2 * n_cut + 2 * n_off, max(nx - 1, 1))),
+        x_r=dma(((2 + n_off) * n_cut, max(nx - 1, 1))),
         s_s=dma((n_off,)),
         s_r=dma((n_off,)),
         z_s=dma((n_off,)),
-        z_r=dma((n_off, 2)),
+        z_r=dma((n_off, n_cut)),
         gx_r=dma((n_cut, max(nx - 1, 1))),
         h_s=dma((2,)),
         h_r=dma((2,)),

time: 24.6 us -> 24.2 us (0.984)
  Pallas kernels: 23.6 us -> 23.2 us
    pallas_call x1, Pallas kernels: 23.6 us -> 23.2 us  [shards(): pl.pallas_call(functools.partial(kernel, dims, names), out_shape=jax.Shap...]
where the time goes in v7:
time: 24.2 us; the launch traced here: 24.1 us
  Pallas kernels  23.2 us (96%)
  other arithmetic  0.85 us (4%)
    pallas_call x1, Pallas kernels, shards(): pl.pallas_call(functools.partial(kernel, dims, names), out_shape=jax.Shap...  23.2 us
    max x1, other arithmetic, shards(): return jnp.maximum(merged_map, jnp.zeros_like(merged_map))  0.85 us

profile of v7, /device:TPU:0, one launch (start us, length us, event | category | flops | bytes accessed | tf_op | source)
XLA Modules:
  0.0 24.1 jit_solution(7858049337054539771)
XLA Ops:
  0.0 23.2 %shard_map.136 = bf16[2,6,96,256]{3,2,1,0:T(8,128)(2,1)S(1)} custom-call(s32[2,6]{1,0:T(2,128)} %refs_0_.1, bf16[2,6,96,512]{3,2,1,0:T(8,128)(2,1)} %refs_1_.1, bf16[2,6,96,256]{3,2,1,0:T(8,128)(2,1)} %refs_2_.1, bf16[512,256]{1,0:T(8,128)(2,1)} %refs_3_.1, bf16[3,3,3,512,256]{4,3,2,1,0:T(8,128)(2,1)} %refs_4_.1, f32[4,256]{1,0:T(4,128)} %refs_5_.1, ...), custom_call_target="tpu_custom_call" | custom-call | tf_op jit(solution)/shard_map/pallas_call | solution.py:795
  23.2 0.9 %broadcast_maximum_fusion = bf16[2,6,96,256]{3,2,1,0:T(8,128)(2,1)} fusion(bf16[2,6,96,256]{3,2,1,0:T(8,128)(2,1)S(1)} %shard_map.136), kind=kLoop, calls=%fused_computation | loop fusion | flops 294912 | bytes 1179648 | tf_op jit(solution)/shard_map/max | solution.py:805

commit v8 on v7

--- a/solution.py
+++ b/solution.py
@@ -29,6 +29,14 @@
     return off
 
 
+def off_slots(off, bands):
+    slots = []
+    for n, (k, i, hop) in enumerate(off):
+        shared = n and off[n - 1][0] == k and 2 * hop >= bands
+        slots.append(slots[-1] if shared else (slots[-1] + 1 if slots else 0))
+    return slots
+
+
 def pieces(live):
     inner = live - 2
     cuts = [(0, 2)]
@@ -48,6 +56,7 @@
     n_off = len(off)
     cuts = pieces(live)
     n_cut = len(cuts)
+    slot_of = off_slots(off, nb)
     need = [(k, 1) for k in ORDER if k] + [(k, i) for k, i, _ in off]
     pad = (r.m_l.shape[1] - cols) // 2
     scope = jax.named_scope
@@ -155,23 +164,23 @@
         if t < 4:
             src, dst = r.part_own.at[t, 0], r.crecv_own.at[t]
         else:
-            src, dst = r.part_off.at[t - 4, 0], r.crecv_off.at[t - 4]
-        return rcopy(src, dst, r.c_s.at[max(t - 3, 0)], r.c_r.at[t], sect=peer)
+            src, dst = r.part_off.at[slot_of[t - 4], 0], r.crecv_off.at[slot_of[t - 4]]
+        return rcopy(src, dst, r.c_s.at[0 if t < 4 else 1 + slot_of[t - 4]], r.c_r.at[t if t < 4 else 4 + slot_of[t - 4]], sect=peer)
 
     def run_of(t, g):
         return cuts[g]
 
     def x_copy(t, g, e, incoming=False):
         lo, n = run_of(t, g)
-        at = g * 2 + t // 3 if t < 4 else (t - 2) * n_cut + g
+        at = g * 2 + t // 3 if t < 4 else (2 + slot_of[t - 4]) * n_cut + g
         send, recv, u = (
-            (r.xsend_own, r.xrecv_own, t) if t < 4 else (r.xsend_off, r.xrecv_off, t - 4)
+            (r.xsend_own, r.xrecv_own, t) if t < 4 else (r.xsend_off, r.xrecv_off, slot_of[t - 4])
         )
         other = lax.rem(xi + e, nx)
         slot = other if incoming else xi
         return rcopy(
             send.at[u, other, pl.ds(lo, n)], recv.at[u, slot, pl.ds(lo, n)],
-            r.x_s.at[max(t - 3, 0)], r.x_r.at[at, (e if incoming else nx - e) - 1],
+            r.x_s.at[0 if t < 4 else 1 + slot_of[t - 4]], r.x_r.at[at, (e if incoming else nx - e) - 1],
             sect=other * 2 + core,
         )
 
@@ -199,7 +208,7 @@
             k, i, _ = off[t - 4]
             lhs = image[...].reshape(rows * cols, ch)
             val = taps(lhs, rows, r.wd.at[need.index((k, i))], DILATIONS[k - 1])
-            r.part_off[t - 4, step] = val.astype(BF16)
+            r.part_off[slot_of[t - 4], step] = val.astype(BF16)
 
     def second(t):
         core_copy(t).wait_recv()
@@ -213,7 +222,7 @@
                 r.keep_own[t] = total
 
     def second_off(t, h):
-        u = t - 4
+        u = slot_of[t - 4]
         if h == 0:
             core_copy(t).wait_recv()
         elif h == 1:
@@ -255,7 +264,7 @@
     def sel_copy(t):
         k, i, hop = off[t - 4]
         return rcopy(
-            r.sel_out, r.sel_in.at[t - 4], r.s_s.at[t - 4], r.s_r.at[t - 4],
+            r.sel_out, r.sel_in.at[slot_of[t - 4]], r.s_s.at[slot_of[t - 4]], r.s_r.at[slot_of[t - 4]],
             band=band - hop if i == 0 else band + hop, sect=sect,
         )
 
@@ -263,17 +272,17 @@
         k, i, hop = off[t - 4]
         run = pl.ds(*cuts[h])
         return rcopy(
-            r.zsend.at[t - 4, run], r.zrecv.at[t - 4, run], r.z_s.at[t - 4], r.z_r.at[t - 4, h],
+            r.zsend.at[slot_of[t - 4], run], r.zrecv.at[slot_of[t - 4], run], r.z_s.at[slot_of[t - 4]], r.z_r.at[slot_of[t - 4], h],
             band=band + hop if i == 0 else band - hop, sect=sect,
         )
 
     def forward_off(t, h):
         run = pl.ds(*cuts[h])
-        total = r.keep_off[t - 4, run]
+        total = r.keep_off[slot_of[t - 4], run]
         for e in range(1, nx):
             x_copy(t, h, e, True).wait_recv()
-            total = total + r.xrecv_off[t - 4, lax.rem(xi + e, nx), run].astype(F32)
-        r.zsend[t - 4, run] = total.astype(BF16)
+            total = total + r.xrecv_off[slot_of[t - 4], lax.rem(xi + e, nx), run].astype(F32)
+        r.zsend[slot_of[t - 4], run] = total.astype(BF16)
         z_copy(t, h).start()
 
     def for_off(fn, *rest):
@@ -536,7 +545,7 @@
                     with scope(f"z{g}"):
                         z_copy(u, g).wait_recv()
                     run = pl.ds(lo, n)
-                    r.keep_own[t, run] = r.keep_own[t, run] + r.zrecv[u - 4, run].astype(F32)
+                    r.keep_own[t, run] = r.keep_own[t, run] + r.zrecv[slot_of[u - 4], run].astype(F32)
         total = r.keep_own[t, lo : lo + n]
         for e in range(1, nx):
             total = total + r.xrecv_own[t, lax.rem(xi + e, nx), lo : lo + n].astype(F32)
@@ -622,39 +631,48 @@
         lower = merge_terms([[rows], [rows + 1]], 1, 2)
         left, mid, right = [jnp.concatenate(p, axis=0) for p in zip(upper, lower)]
         r.lowacc[:2] = r.lowacc[:2] + combine(mid, left, right, 2)
-    with scope("gb"):
-        for g in range(1, n_cut):
+    def merged_copy(lo, n):
+        run = pl.ds(lo, n)
+        return rcopy(
+            r.merged.at[run], r.merged_in.at[run], r.one_s.at[3], r.one_r.at[2], sect=peer
+        )
+
+    def finish(lo, n, terms):
+        left, mid, right = terms
+        total = combine(mid, left, right, n) + r.lowacc[lo : lo + n]
+        r.merged[lo : lo + n] = jax.nn.relu(total).astype(BF16)
+        merged_copy(lo, n).start()
+
+    def gathered(g):
+        with scope(f"gb{g}"):
             for e in range(1, nx):
                 gather_x(g, e, True).wait_recv()
+
+    def join(y, c, p):
+        r.joined[y + 1, pl.ds(c * cs, cs)] = (
+            r.gath[c, p].astype(F32) * on[y].astype(F32)
+        ).astype(BF16)
+
+    if n_cut > 1:
+        gathered(1)
+    for c in range(nx):
+        join(1, c, min(2, live - 1))
+    with scope("merge0"):
+        finish(0, 1, merge_terms([[2]], 2, 1))
+    for g in range(2, n_cut):
+        gathered(g)
     with scope("join"):
-        for y in range(1, rows - 1):
+        for y in range(2, rows - 1):
             for c in range(nx):
-                r.joined[y + 1, pl.ds(c * cs, cs)] = (
-                    r.gath[c, place_of[y]].astype(F32) * on[y].astype(F32)
-                ).astype(BF16)
-
-    def merged_copy(h):
-        run = pl.ds(*halves[h])
-        return rcopy(
-            r.merged.at[run], r.merged_in.at[run], r.one_s.at[3], r.one_r.at[2], sect=peer
-        )
-
-    halves = [(2, live - 2), (0, 2)] if live > 2 else [(0, 2)]
-    for h, (lo, n) in enumerate(halves):
-        with scope(f"merge{h}"):
-            if lo:
-                terms = merge_terms(
-                    [[row_of[p] + i for p in range(lo, lo + n)] for i in range(3)], 0, 3
-                )
-            else:
-                terms = [
-                    jnp.concatenate(p, axis=0)
-                    for p in zip(merge_terms([[2]], 2, 1), merge_terms([[rows - 1]], 0, 1))
-                ]
-            left, mid, right = terms
-            total = combine(mid, left, right, n) + r.lowacc[lo : lo + n]
-            r.merged[lo : lo + n] = jax.nn.relu(total).astype(BF16)
-        merged_copy(h).start()
+                join(y, c, place_of[y])
+    if live > 2:
+        with scope("merge1"):
+            inner = range(2, live)
+            finish(
+                2, live - 2, merge_terms([[row_of[p] + i for p in inner] for i in range(3)], 0, 3)
+            )
+    with scope("merge2"):
+        finish(1, 1, merge_terms([[rows - 1]], 0, 1))
 
     def spread(image, src, flags, places):
         for y in range(rows):
@@ -676,7 +694,7 @@
         low_dn.wait_send()
 
     def off_sent(t):
-        u = t - 4
+        u = slot_of[t - 4]
         core_copy(t).wait_send()
         if nx > 1:
             arrived(all_of(r.xsend_off.at[u], nx - 1), r.x_s.at[1 + u])
@@ -716,7 +734,7 @@
     assert mb == 2 and ns % 2 == 0 and rows > 2
     live = rows // LAND_BLOCK * LAND_MOST if rows % LAND_BLOCK == 0 else rows
     off = offsets(rows, nb)
-    n_off = max(len(off), 1)
+    n_off = max(off_slots(off, nb), default=0) + 1
     assert dec == br_w
     n_cut = len(pieces(live))
     n_sel = -(-(live - 2) * (rows - 2) // 8) * 8

time: 24.2 us -> 24 us (level)
  no operation moved by 1% of the time
where the time goes in v8:
time: 24 us; the launch traced here: 23.9 us
  Pallas kernels  23 us (96%)
  other arithmetic  0.85 us (4%)
    pallas_call x1, Pallas kernels, shards(): pl.pallas_call(functools.partial(kernel, dims, names), out_shape=jax.Shap...  23 us
    max x1, other arithmetic, shards(): return jnp.maximum(merged_map, jnp.zeros_like(merged_map))  0.85 us

profile of v8, /device:TPU:0, one launch (start us, length us, event | category | flops | bytes accessed | tf_op | source)
XLA Modules:
  0.0 23.9 jit_solution(981771118745624683)
XLA Ops:
  0.0 23.0 %shard_map.136 = bf16[2,6,96,256]{3,2,1,0:T(8,128)(2,1)S(1)} custom-call(s32[2,6]{1,0:T(2,128)} %refs_0_.1, bf16[2,6,96,512]{3,2,1,0:T(8,128)(2,1)} %refs_1_.1, bf16[2,6,96,256]{3,2,1,0:T(8,128)(2,1)} %refs_2_.1, bf16[512,256]{1,0:T(8,128)(2,1)} %refs_3_.1, bf16[3,3,3,512,256]{4,3,2,1,0:T(8,128)(2,1)} %refs_4_.1, f32[4,256]{1,0:T(4,128)} %refs_5_.1, ...), custom_call_target="tpu_custom_call" | custom-call | tf_op jit(solution)/shard_map/pallas_call | solution.py:813
  23.0 0.9 %broadcast_maximum_fusion = bf16[2,6,96,256]{3,2,1,0:T(8,128)(2,1)} fusion(bf16[2,6,96,256]{3,2,1,0:T(8,128)(2,1)S(1)} %shard_map.136), kind=kLoop, calls=%fused_computation | loop fusion | flops 294912 | bytes 1179648 | tf_op jit(solution)/shard_map/max | solution.py:823

commit v9 on v8

--- a/solution.py
+++ b/solution.py
@@ -83,9 +83,10 @@
             hello(band + step, sect)
 
     waits = {}
+    free = list(range(r.loc_sem.shape[0]))
 
     def fetch(name, *copies, whole):
-        sem = r.loc_sem.at[len(waits)]
+        sem = r.loc_sem.at[free.pop(0)]
         for src, dst in copies:
             pltpu.make_async_copy(src, dst, sem).start()
         waits[name] = pltpu.make_async_copy(whole, whole, sem)
@@ -358,9 +359,9 @@
 
     with scope("w0"):
         need_now("theirs", "w1")
+    free[:0] = range(3)
     fetch("wpool", (r.wpool_h, r.wpool), whole=r.wpool)
-    fetch("taps0", taps_of(*need[0]), whole=r.wd.at[0])
-    fetch("taps1", *[taps_of(*n) for n in need[1:3]], whole=r.wd.at[pl.ds(1, 2)])
+    fetch("taps", *[taps_of(*n) for n in need[:3]], whole=r.wd.at[pl.ds(0, 3)])
     fetch("low", (r.low_h.at[mine], r.low), whole=r.low)
     fetch("wr", (r.wr_h, r.wr), whole=r.wr)
     fetch("br", (r.br_h, r.br), whole=r.br)
@@ -432,7 +433,7 @@
         for_off(off_send, 0)
     for g in range(1, n_cut):
         send_x(0, g)
-    need_now("taps0", "taps1")
+    need_now("taps")
     own_half(1, 0)
     own_half(2, 0)
     with scope("p3"):
@@ -561,7 +562,7 @@
         slot = other if incoming else xi
         return rcopy(
             r.gath.at[xi, run], r.gath.at[slot, run],
-            r.one_s.at[2], r.gx_r.at[g, (e if incoming else nx - e) - 1], sect=other * 2 + core,
+            r.x_s.at[0], r.gx_r.at[g, (e if incoming else nx - e) - 1], sect=other * 2 + core,
         )
 
     def early(g):
@@ -594,9 +595,17 @@
     def halo_copy(side, e):
         other = lax.rem(xi + e, nx)
         return rcopy(
-            r.gath.at[xi, 1 - side], r.halo.at[side, xi], r.h_s.at[side], r.h_r.at[side],
+            r.gath.at[xi, 1 - side], r.halo.at[side, xi], r.lo_s.at[1 - side], r.h_r.at[side],
             band=band + 1 if side == 0 else band - 1, sect=other * 2 + core,
         )
+
+    @pl.when(up_ok)
+    def _():
+        low_up.wait_send()
+
+    @pl.when(dn_ok)
+    def _():
+        low_dn.wait_send()
 
     early(0)
     project(0)
@@ -634,7 +643,7 @@
     def merged_copy(lo, n):
         run = pl.ds(lo, n)
         return rcopy(
-            r.merged.at[run], r.merged_in.at[run], r.one_s.at[3], r.one_r.at[2], sect=peer
+            r.merged.at[run], r.merged_in.at[run], r.c_s.at[0], r.c_r.at[0], sect=peer
         )
 
     def finish(lo, n, terms):
@@ -681,17 +690,9 @@
     with scope("spread"):
         spread(mine, r.merged, on, place_of)
     with scope("ow"):
-        arrived(r.merged, r.one_r.at[2])
+        arrived(r.merged, r.c_r.at[0])
     with scope("spread2"):
         spread(theirs, r.merged_in, facts[0][0], facts[0][1])
-
-    @pl.when(up_ok)
-    def _():
-        low_up.wait_send()
-
-    @pl.when(dn_ok)
-    def _():
-        low_dn.wait_send()
 
     def off_sent(t):
         u = slot_of[t - 4]
@@ -708,15 +709,13 @@
     arrived(r.part_own.at[:, 0], r.c_s.at[0])
     if nx > 1:
         arrived(r.xsend_own.at[:, pl.ds(0, nx - 1)], r.x_s.at[0])
-        arrived(all_of(r.gath, nx - 1), r.one_s.at[2])
     arrived(all_of(r.pool_s, ns - 1), r.one_s.at[0])
     if nb > 1:
         arrived(all_of(r.pool_b, nb - 1), r.one_s.at[1])
     for side, ok in ((0, dn_ok), (1, up_ok)):
         @pl.when(ok)
         def _(side=side):
-            arrived(r.halo.at[side], r.h_s.at[side])
-    arrived(r.merged, r.one_s.at[3])
+            arrived(r.halo.at[side], r.lo_s.at[1 - side])
 
 
 def shards(
@@ -774,9 +773,9 @@
         zsend=vm((n_off, live, cs, br_w), BF16),
         zrecv=vm((n_off, live, cs, br_w), BF16),
         keep_off=vm((n_off, live, cs, br_w), F32),
-        part_own=vm((4, 2, live, cols, br_w), BF16),
+        part_own=vm((5, 2, live, cols, br_w), BF16),
         crecv_own=vm((4, live, cols, br_w), BF16),
-        xsend_own=vm((4, nx, live, cs, br_w), BF16),
+        xsend_own=vm((5, nx, live, cs, br_w), BF16),
         xrecv_own=vm((4, nx, live, cs, br_w), BF16),
         keep_own=vm((4, live, cs, br_w), F32),
         acc=vm((live, cs, br_w), F32),
@@ -792,9 +791,9 @@
         across=pltpu.SemaphoreType.REGULAR,
         above=pltpu.SemaphoreType.REGULAR,
         below=pltpu.SemaphoreType.REGULAR,
-        loc_sem=dma((16,)),
-        one_s=dma((4,)),
-        one_r=dma((3,)),
+        loc_sem=dma((12,)),
+        one_s=dma((2,)),
+        one_r=dma((2,)),
         lo_s=dma((2,)),
         lo_r=dma((2,)),
         c_s=dma((1 + n_off,)),
@@ -806,7 +805,6 @@
         z_s=dma((n_off,)),
         z_r=dma((n_off, n_cut)),
         gx_r=dma((n_cut, max(nx - 1, 1))),
-        h_s=dma((2,)),
         h_r=dma((2,)),
     )
     names = (*args, "out", *scratch)

time: 24 us -> 23.9 us (level)
  no operation moved by 1% of the time
where the time goes in v9:
time: 23.9 us; the launch traced here: 23.8 us
  Pallas kernels  22.9 us (96%)
  other arithmetic  0.85 us (4%)
    pallas_call x1, Pallas kernels, shards(): pl.pallas_call(functools.partial(kernel, dims, names), out_shape=jax.Shap...  22.9 us
    max x1, other arithmetic, shards(): return jnp.maximum(merged_map, jnp.zeros_like(merged_map))  0.85 us

profile of v9, /device:TPU:0, one launch (start us, length us, event | category | flops | bytes accessed | tf_op | source)
XLA Modules:
  0.0 23.8 jit_solution(5417301883742678539)
XLA Ops:
  0.0 22.9 %shard_map.136 = bf16[2,6,96,256]{3,2,1,0:T(8,128)(2,1)S(1)} custom-call(s32[2,6]{1,0:T(2,128)} %refs_0_.1, bf16[2,6,96,512]{3,2,1,0:T(8,128)(2,1)} %refs_1_.1, bf16[2,6,96,256]{3,2,1,0:T(8,128)(2,1)} %refs_2_.1, bf16[512,256]{1,0:T(8,128)(2,1)} %refs_3_.1, bf16[3,3,3,512,256]{4,3,2,1,0:T(8,128)(2,1)} %refs_4_.1, f32[4,256]{1,0:T(4,128)} %refs_5_.1, ...), custom_call_target="tpu_custom_call" | custom-call | tf_op jit(solution)/shard_map/pallas_call | solution.py:811
  22.9 0.9 %broadcast_maximum_fusion = bf16[2,6,96,256]{3,2,1,0:T(8,128)(2,1)} fusion(bf16[2,6,96,256]{3,2,1,0:T(8,128)(2,1)S(1)} %shard_map.136), kind=kLoop, calls=%fused_computation | loop fusion | flops 294912 | bytes 1179648 | tf_op jit(solution)/shard_map/max | solution.py:821

commit v10 on v9

--- a/solution.py
+++ b/solution.py
@@ -370,6 +370,41 @@
         "vec", (r.bm_h, r.vec.at[0]), (r.bpool_h, r.vec.at[1]), (r.bproj_h, r.vec.at[2]),
         whole=r.vec,
     )
+    with scope("first0a"):
+        first(0, 0)
+    with scope("bar"):
+        sides = jnp.minimum(band, 1) + jnp.minimum(nb - 1 - band, 1)
+        pl.semaphore_wait(bar, (ns - 1) + sides)
+    core_copy(0).start()
+    for e in range(1, nx):
+        pl.semaphore_signal(
+            r.across, inc=1, device_id={"sect": lax.rem(sect + 2 * e, ns)}, device_id_type=MESH
+        )
+    pass_on(r.above, 1, band < 2)
+    pass_on(r.below, -1, band + 2 >= nb)
+
+    def tell(i, ok):
+        for t in range(4, 4 + n_off):
+            if off[t - 4][1] == i:
+                @pl.when(jnp.logical_and(gets_from(t), ok))
+                def _(t=t):
+                    sel_copy(t).start()
+
+    @pl.when(up_ok)
+    def _():
+        low_up.start()
+
+    @pl.when(dn_ok)
+    def _():
+        low_dn.start()
+
+    need_now("mine")
+    own_half(0, 1)
+    if n_off:
+        need_now("off")
+    with scope("offa"):
+        for_off(off_theirs)
+    free[:0] = [3, 4] if n_off else [3]
     fetch("wproj", (r.wproj_h, r.wproj), whole=r.wproj)
     fetch("bbr", (r.bbr_h, r.bbr), whole=r.bbr)
     fetch(
@@ -380,40 +415,6 @@
         ],
         whole=r.wmp,
     )
-    with scope("first0a"):
-        first(0, 0)
-    with scope("bar"):
-        sides = jnp.minimum(band, 1) + jnp.minimum(nb - 1 - band, 1)
-        pl.semaphore_wait(bar, (ns - 1) + sides)
-    core_copy(0).start()
-    for e in range(1, nx):
-        pl.semaphore_signal(
-            r.across, inc=1, device_id={"sect": lax.rem(sect + 2 * e, ns)}, device_id_type=MESH
-        )
-    pass_on(r.above, 1, band < 2)
-    pass_on(r.below, -1, band + 2 >= nb)
-
-    def tell(i, ok):
-        for t in range(4, 4 + n_off):
-            if off[t - 4][1] == i:
-                @pl.when(jnp.logical_and(gets_from(t), ok))
-                def _(t=t):
-                    sel_copy(t).start()
-
-    @pl.when(up_ok)
-    def _():
-        low_up.start()
-
-    @pl.when(dn_ok)
-    def _():
-        low_dn.start()
-
-    need_now("mine")
-    own_half(0, 1)
-    if n_off:
-        need_now("off")
-    with scope("offa"):
-        for_off(off_theirs)
     with scope("second0"):
         second(0)
     send_x(0, 0)
@@ -791,7 +792,7 @@
         across=pltpu.SemaphoreType.REGULAR,
         above=pltpu.SemaphoreType.REGULAR,
         below=pltpu.SemaphoreType.REGULAR,
-        loc_sem=dma((12,)),
+        loc_sem=dma((10,)),
         one_s=dma((2,)),
         one_r=dma((2,)),
         lo_s=dma((2,)),

time: 23.9 us -> 23.9 us (level)
  no operation moved by 1% of the time
where the time goes in v10:
time: 23.9 us; the launch traced here: 23.8 us
  Pallas kernels  22.9 us (96%)
  other arithmetic  0.85 us (4%)
    pallas_call x1, Pallas kernels, shards(): pl.pallas_call(functools.partial(kernel, dims, names), out_shape=jax.Shap...  22.9 us
    max x1, other arithmetic, shards(): return jnp.maximum(merged_map, jnp.zeros_like(merged_map))  0.85 us

profile of v10, /device:TPU:0, one launch (start us, length us, event | category | flops | bytes accessed | tf_op | source)
XLA Modules:
  0.0 23.8 jit_solution(2134022699984691253)
XLA Ops:
  0.0 22.9 %shard_map.136 = bf16[2,6,96,256]{3,2,1,0:T(8,128)(2,1)S(1)} custom-call(s32[2,6]{1,0:T(2,128)} %refs_0_.1, bf16[2,6,96,512]{3,2,1,0:T(8,128)(2,1)} %refs_1_.1, bf16[2,6,96,256]{3,2,1,0:T(8,128)(2,1)} %refs_2_.1, bf16[512,256]{1,0:T(8,128)(2,1)} %refs_3_.1, bf16[3,3,3,512,256]{4,3,2,1,0:T(8,128)(2,1)} %refs_4_.1, f32[4,256]{1,0:T(4,128)} %refs_5_.1, ...), custom_call_target="tpu_custom_call" | custom-call | tf_op jit(solution)/shard_map/pallas_call | solution.py:812
  22.9 0.9 %broadcast_maximum_fusion = bf16[2,6,96,256]{3,2,1,0:T(8,128)(2,1)} fusion(bf16[2,6,96,256]{3,2,1,0:T(8,128)(2,1)S(1)} %shard_map.136), kind=kLoop, calls=%fused_computation | loop fusion | flops 294912 | bytes 1179648 | tf_op jit(solution)/shard_map/max | solution.py:822
